TPU v7x, 32 devices: a whole 2x2x4 slice. The times are simulated.
32 devices in a mesh: seq: 8 (over z, x), chan: 4 (over y, core).
Axes of the slice: x: 2, y: 2, z: 4, core: 2. Of those that a mesh axis runs over, the one named last changes fastest.
Arguments:
- projected: bfloat16 [1024, 3, 2048], P('seq', None, 'chan'), may hold values from -6 to 6
- short_filter: bfloat16 [3, 16, 3], P(None, 'chan'), may hold values from -3.5 to 3.5
- long_filter: bfloat16 [16, 768], P('chan', 'seq'), may hold values from -0.21875 to 0.21875
- out_weight: bfloat16 [2048, 2048], P('chan'), may hold values from -0.125 to 0.125
Outputs:
- mixer_out: bfloat16 [1024, 2048], P(('seq', 'chan'))
All inputs are finite; a program needn't handle non-finite values.
Results may differ from a plain program's by a relative error of at most 0.0057.
Values may be sent and summed in bfloat16 or wider, within the bound.
No kernel may reach another device: no remote copies, remote signals or barrier semaphores. Data moves between devices by JAX's collectives and lax.ppermute only.
A program may use at most 64 MiB of HBM per device.

v0:
```python
import jax
import jax.numpy as jnp
from jax import lax
from jax.sharding import PartitionSpec as P

REACH = 6


def shifted(array, axis, by):
    peers = lax.axis_size(axis)
    pairs = [(i, i + by) for i in range(peers) if 0 <= i + by < peers]
    return lax.ppermute(array, axis, pairs)


def toeplitz_block(padded, offset, row_count):
    group_count = padded.shape[0]
    window = lax.slice_in_dim(
        padded, offset * row_count + 1, offset * row_count + 2 * row_count, axis=1
    )
    tiled_rows = jnp.tile(window, (1, row_count + 1))[:, : 2 * row_count * row_count]
    tiled_rows = tiled_rows.reshape(group_count, row_count, 2 * row_count)
    return tiled_rows[:, :, :row_count][:, :, ::-1]


def on_device(projected, short_filter, long_filter, out_weight):
    row_count, _, chan_count = projected.shape
    tap_count = short_filter.shape[-1]
    group_count = short_filter.shape[1]
    group_width = chan_count // group_count
    tail_rows = projected[row_count - tap_count + 1 :]
    arrived_rim = shifted(tail_rows, "seq", 1)
    padded_rows = jnp.concatenate([arrived_rim, projected], axis=0)
    channel_taps = jnp.repeat(short_filter.astype(jnp.float32), group_width, axis=1)
    streams = jnp.zeros((row_count, 3, chan_count), jnp.float32)
    for lag in range(tap_count):
        begin = tap_count - 1 - lag
        window = lax.slice_in_dim(padded_rows, begin, begin + row_count, axis=0)
        streams = streams + channel_taps[None, :, :, lag] * window.astype(jnp.float32)
    query_part = streams[:, 0]
    gated_input = (streams[:, 1] * streams[:, 2]).astype(jnp.bfloat16)
    filters = lax.all_gather(long_filter, "seq", axis=1, tiled=True)
    padded = jnp.pad(filters, ((0, 0), (row_count, row_count)))

    def add_offset(running, offset, source_block):
        matrix = toeplitz_block(padded, offset, row_count)
        shaped_block = source_block.reshape(row_count, group_count, group_width)
        return running + jnp.einsum(
            "gij,jgc->igc", matrix, shaped_block, preferred_element_type=jnp.float32
        )

    running = add_offset(
        jnp.zeros((row_count, group_count, group_width), jnp.float32), 0, gated_input
    )
    moving = gated_input
    for offset in range(1, REACH + 1):
        moving = shifted(moving, "seq", 1)
        running = add_offset(running, offset, moving)
    mixed_out = (query_part * running.reshape(row_count, chan_count)).astype(jnp.bfloat16)
    result = lax.psum_scatter(
        jnp.dot(mixed_out, out_weight, preferred_element_type=jnp.float32),
        "chan",
        scatter_dimension=0,
        tiled=True,
    )
    return result.astype(jnp.bfloat16)


def solution(mesh):
    return jax.shard_map(
        on_device,
        mesh=mesh,
        in_specs=(P("seq", None, "chan"), P(None, "chan", None), P("chan", "seq"), P("chan", None)),
        out_specs=P(("seq", "chan"), None),
        check_vma=False,
    )
```

profile of v0, /device:TPU:0, one launch (start us, length us, event | category | flops | bytes accessed | tf_op | source)
XLA Modules:
  0.0 140.7 jit_solution(4365507923990612729)
XLA Ops:
  7.4 4.9 %collective-permute-start = (bf16[2,3,512]{2,0,1:T(2,128)(2,1)S(1)}, bf16[2,3,512]{2,0,1:T(2,128)(2,1)S(1)}, u32[]{:S(2)}, u32[]{:S(2)}) collective-permute-start(bf16[2,3,512]{2,0,1:T(2,128)(2,1)S(1)} %slice.97), channel_id=1, source_target_pairs={{0,4},{4,8},{8,12},{12,16},{16,20},{20,24},{24,28},{1,5},{5,9},{9,... | collective-permute-start | bytes 18440 | tf_op jit(solution)/shard_map/ppermute | solution.py:12
  13.2 19.0 %all-gather = bf16[8,96,4]{1,2,0:T(4,128)(2,1)S(1)} all-gather(bf16[1,96,4]{1,2,0:T(4,128)(2,1)} %bitcast.99), channel_id=1, replica_groups=mesh['seq'=8,'chan'=4] {'seq'}, dimensions={0}, use_global_device_ids=true | all-gather | bytes 6912 | tf_op jit(solution)/shard_map/all_gather | solution.py:41
  34.2 1.5 %rev.22 = bf16[4,128,128]{2,1,0:T(8,128)(2,1)} reverse(bf16[4,128,128]{2,1,0:T(8,128)(2,1)S(1)} %slice.137), dimensions={2} | reverse | bytes 262144 | tf_op jit(solution)/shard_map/rev | solution.py:22
  36.5 1.5 %rev.23 = bf16[4,128,128]{2,1,0:T(8,128)(2,1)} reverse(bf16[4,128,128]{2,1,0:T(8,128)(2,1)S(1)} %slice.140), dimensions={2} | reverse | bytes 262144 | tf_op jit(solution)/shard_map/rev | solution.py:22
  38.7 1.5 %rev.24 = bf16[4,128,128]{2,1,0:T(8,128)(2,1)} reverse(bf16[4,128,128]{2,1,0:T(8,128)(2,1)S(1)} %slice.143), dimensions={2} | reverse | bytes 262144 | tf_op jit(solution)/shard_map/rev | solution.py:22
  40.9 1.5 %rev.25 = bf16[4,128,128]{2,1,0:T(8,128)(2,1)} reverse(bf16[4,128,128]{2,1,0:T(8,128)(2,1)S(1)} %slice.146), dimensions={2} | reverse | bytes 262144 | tf_op jit(solution)/shard_map/rev | solution.py:22
  44.3 1.5 %rev.27 = bf16[4,128,128]{2,1,0:T(8,128)(2,1)} reverse(bf16[4,128,128]{2,1,0:T(8,128)(2,1)S(1)} %slice.151), dimensions={2} | reverse | bytes 262144 | tf_op jit(solution)/shard_map/rev | solution.py:22
  45.8 1.6 %multiply_add_fusion = f32[128,3,512]{2,0,1:T(8,128)S(1)} fusion(bf16[128,3,512]{2,0,1:T(8,128)(2,1)} %param.4, bf16[2,3,512]{2,0,1:T(2,128)(2,1)S(1)} %collective-permute-done, f32[3,512]{1,0:T(4,128)S(1)} %get-tuple-element.6, f32[3,512]{1,0:T(4,128)S(1)} %get-tuple-element.7, f32[3,512]{1,0:T(4,128)S(1)} %get-tuple-element.5), kind=kLoop, calls=%fused_computation.6 | loop fusion | flops 2752512 | bytes 1204224 | tf_op jit(solution)/shard_map/add | solution.py:38
  48.9 2.5 %collective-permute-start.1 = (bf16[128,512]{1,0:T(8,128)(2,1)}, bf16[128,512]{1,0:T(8,128)(2,1)}, u32[]{:S(2)}, u32[]{:S(2)}) collective-permute-start(bf16[128,512]{1,0:T(8,128)(2,1)} %fusion.22), channel_id=1, source_target_pairs={{0,4},{4,8},{8,12},{12,16},{16,20},{20,24},{24,28},{1,5},{5,9},{9,... | collective-permute-start | bytes 393224 | tf_op jit(solution)/shard_map/ppermute | solution.py:12
  53.5 1.7 %copy.27 = bf16[128,512]{0,1:T(8,128)(2,1)} copy(bf16[128,512]{1,0:T(8,128)(2,1)} %collective-permute-done.1) | data formatting | bytes 262144 | tf_op jit(solution)/shard_map/ppermute | solution.py:12
  55.2 5.0 %collective-permute-start.2 = (bf16[128,512]{1,0:T(8,128)(2,1)}, bf16[128,512]{1,0:T(8,128)(2,1)}, u32[]{:S(2)}, u32[]{:S(2)}) collective-permute-start(bf16[128,512]{1,0:T(8,128)(2,1)} %collective-permute-done.1), channel_id=1, source_target_pairs={{0,4},{4,8},{8,12},{12,16},{16,20},{20,24},{24,28},{1,5},{5,9},{9,... | collective-permute-start | bytes 393224 | tf_op jit(solution)/shard_map/ppermute | solution.py:12
  62.3 1.7 %copy.28 = bf16[128,512]{0,1:T(8,128)(2,1)} copy(bf16[128,512]{1,0:T(8,128)(2,1)} %collective-permute-done.2) | data formatting | bytes 262144 | tf_op jit(solution)/shard_map/ppermute | solution.py:12
  64.0 5.0 %collective-permute-start.3 = (bf16[128,512]{1,0:T(8,128)(2,1)}, bf16[128,512]{1,0:T(8,128)(2,1)}, u32[]{:S(2)}, u32[]{:S(2)}) collective-permute-start(bf16[128,512]{1,0:T(8,128)(2,1)} %collective-permute-done.2), channel_id=1, source_target_pairs={{0,4},{4,8},{8,12},{12,16},{16,20},{20,24},{24,28},{1,5},{5,9},{9,... | collective-permute-start | bytes 393224 | tf_op jit(solution)/shard_map/ppermute | solution.py:12
  70.2 1.9 %collective-permute-done.3 = bf16[128,512]{1,0:T(8,128)(2,1)} collective-permute-done((bf16[128,512]{1,0:T(8,128)(2,1)}, bf16[128,512]{1,0:T(8,128)(2,1)}, u32[]{:S(2)}, u32[]{:S(2)}) %collective-permute-start.3) | collective-permute-done | bytes 131104 | tf_op jit(solution)/shard_map/ppermute | solution.py:12
  72.1 1.7 %copy.29 = bf16[128,512]{0,1:T(8,128)(2,1)} copy(bf16[128,512]{1,0:T(8,128)(2,1)} %collective-permute-done.3) | data formatting | bytes 262144 | tf_op jit(solution)/shard_map/ppermute | solution.py:12
  73.7 5.0 %collective-permute-start.4 = (bf16[128,512]{1,0:T(8,128)(2,1)}, bf16[128,512]{1,0:T(8,128)(2,1)}, u32[]{:S(2)}, u32[]{:S(2)}) collective-permute-start(bf16[128,512]{1,0:T(8,128)(2,1)} %collective-permute-done.3), channel_id=1, source_target_pairs={{0,4},{4,8},{8,12},{12,16},{16,20},{20,24},{24,28},{1,5},{5,9},{9,... | collective-permute-start | bytes 393224 | tf_op jit(solution)/shard_map/ppermute | solution.py:12
  79.9 1.7 %collective-permute-done.4 = bf16[128,512]{1,0:T(8,128)(2,1)} collective-permute-done((bf16[128,512]{1,0:T(8,128)(2,1)}, bf16[128,512]{1,0:T(8,128)(2,1)}, u32[]{:S(2)}, u32[]{:S(2)}) %collective-permute-start.4) | collective-permute-done | bytes 131104 | tf_op jit(solution)/shard_map/ppermute | solution.py:12
  81.6 1.7 %copy.30 = bf16[128,512]{0,1:T(8,128)(2,1)} copy(bf16[128,512]{1,0:T(8,128)(2,1)} %collective-permute-done.4) | data formatting | bytes 262144 | tf_op jit(solution)/shard_map/ppermute | solution.py:12
  83.3 5.1 %collective-permute-start.5 = (bf16[128,512]{1,0:T(8,128)(2,1)}, bf16[128,512]{1,0:T(8,128)(2,1)}, u32[]{:S(2)}, u32[]{:S(2)}) collective-permute-start(bf16[128,512]{1,0:T(8,128)(2,1)} %collective-permute-done.4), channel_id=1, source_target_pairs={{0,4},{4,8},{8,12},{12,16},{16,20},{20,24},{24,28},{1,5},{5,9},{9,... | collective-permute-start | bytes 393224 | tf_op jit(solution)/shard_map/ppermute | solution.py:12
  89.5 1.7 %collective-permute-done.5 = bf16[128,512]{1,0:T(8,128)(2,1)} collective-permute-done((bf16[128,512]{1,0:T(8,128)(2,1)}, bf16[128,512]{1,0:T(8,128)(2,1)}, u32[]{:S(2)}, u32[]{:S(2)}) %collective-permute-start.5) | collective-permute-done | bytes 131104 | tf_op jit(solution)/shard_map/ppermute | solution.py:12
  91.3 1.7 %copy.31 = bf16[128,512]{0,1:T(8,128)(2,1)} copy(bf16[128,512]{1,0:T(8,128)(2,1)} %collective-permute-done.5) | data formatting | bytes 262144 | tf_op jit(solution)/shard_map/ppermute | solution.py:12
  93.0 5.7 %collective-permute-start.6 = (bf16[128,512]{1,0:T(8,128)(2,1)}, bf16[128,512]{1,0:T(8,128)(2,1)}, u32[]{:S(2)}, u32[]{:S(2)}) collective-permute-start(bf16[128,512]{1,0:T(8,128)(2,1)} %collective-permute-done.5), channel_id=1, source_target_pairs={{0,4},{4,8},{8,12},{12,16},{16,20},{20,24},{24,28},{1,5},{5,9},{9,... | collective-permute-start | bytes 393224 | tf_op jit(solution)/shard_map/ppermute | solution.py:12
  104.6 27.6 %reduce-scatter.2.cloned.1.call-done = f32[32,2048]{1,0:T(8,128)} async-done(((f32[128,2048]{1,0:T(8,128)}), f32[32,2048]{1,0:T(8,128)}) %reduce-scatter.2.cloned.1.call-update) | async-done | bytes 262160 | tf_op jit(solution)/shard_map/reduce_scatter | solution.py:59
  132.2 1.6 %convert_element_type.38 = bf16[32,2048]{1,0:T(8,128)(2,1)} convert(f32[32,2048]{1,0:T(8,128)} %reduce-scatter.2.cloned.1.call-done) | non-fusion elementwise | flops 65536 | bytes 393216 | tf_op jit(solution)/shard_map/convert_element_type | solution.py:65
  (66 shorter events, 22.8 us)
Async XLA Ops:
  6.5 96.6 %copy-start = (bf16[512,2048]{1,0:T(8,128)(2,1)S(1)}, bf16[512,2048]{1,0:T(8,128)(2,1)}, u32[]{:S(2)}) copy-start(bf16[512,2048]{1,0:T(8,128)(2,1)} %param.7) | copy-start | bytes 6291460
  6.5 125.6 %reduce-scatter.2.cloned.1.call-start = ((), (), s32[]{:S(2)}) async-start(), calls=%async_computation.1 | async-start | bytes 1310720 | tf_op jit(solution)/shard_map/reduce_scatter | solution.py:59
  7.4 38.4 %collective-permute-start = (bf16[2,3,512]{2,0,1:T(2,128)(2,1)S(1)}, bf16[2,3,512]{2,0,1:T(2,128)(2,1)S(1)}, u32[]{:S(2)}, u32[]{:S(2)}) collective-permute-start(bf16[2,3,512]{2,0,1:T(2,128)(2,1)S(1)} %slice.97), channel_id=1, source_target_pairs={{0,4},{4,8},{8,12},{12,16},{16,20},{20,24},{24,28},{1,5},{5,9},{9,... | collective-permute-start | bytes 18440 | tf_op jit(solution)/shard_map/ppermute | solution.py:12
  48.9 4.6 %collective-permute-start.1 = (bf16[128,512]{1,0:T(8,128)(2,1)}, bf16[128,512]{1,0:T(8,128)(2,1)}, u32[]{:S(2)}, u32[]{:S(2)}) collective-permute-start(bf16[128,512]{1,0:T(8,128)(2,1)} %fusion.22), channel_id=1, source_target_pairs={{0,4},{4,8},{8,12},{12,16},{16,20},{20,24},{24,28},{1,5},{5,9},{9,... | collective-permute-start | bytes 393224 | tf_op jit(solution)/shard_map/ppermute | solution.py:12
  55.2 7.2 %collective-permute-start.2 = (bf16[128,512]{1,0:T(8,128)(2,1)}, bf16[128,512]{1,0:T(8,128)(2,1)}, u32[]{:S(2)}, u32[]{:S(2)}) collective-permute-start(bf16[128,512]{1,0:T(8,128)(2,1)} %collective-permute-done.1), channel_id=1, source_target_pairs={{0,4},{4,8},{8,12},{12,16},{16,20},{20,24},{24,28},{1,5},{5,9},{9,... | collective-permute-start | bytes 393224 | tf_op jit(solution)/shard_map/ppermute | solution.py:12
  64.0 8.1 %collective-permute-start.3 = (bf16[128,512]{1,0:T(8,128)(2,1)}, bf16[128,512]{1,0:T(8,128)(2,1)}, u32[]{:S(2)}, u32[]{:S(2)}) collective-permute-start(bf16[128,512]{1,0:T(8,128)(2,1)} %collective-permute-done.2), channel_id=1, source_target_pairs={{0,4},{4,8},{8,12},{12,16},{16,20},{20,24},{24,28},{1,5},{5,9},{9,... | collective-permute-start | bytes 393224 | tf_op jit(solution)/shard_map/ppermute | solution.py:12
  73.7 7.9 %collective-permute-start.4 = (bf16[128,512]{1,0:T(8,128)(2,1)}, bf16[128,512]{1,0:T(8,128)(2,1)}, u32[]{:S(2)}, u32[]{:S(2)}) collective-permute-start(bf16[128,512]{1,0:T(8,128)(2,1)} %collective-permute-done.3), channel_id=1, source_target_pairs={{0,4},{4,8},{8,12},{12,16},{16,20},{20,24},{24,28},{1,5},{5,9},{9,... | collective-permute-start | bytes 393224 | tf_op jit(solution)/shard_map/ppermute | solution.py:12
  83.3 8.0 %collective-permute-start.5 = (bf16[128,512]{1,0:T(8,128)(2,1)}, bf16[128,512]{1,0:T(8,128)(2,1)}, u32[]{:S(2)}, u32[]{:S(2)}) collective-permute-start(bf16[128,512]{1,0:T(8,128)(2,1)} %collective-permute-done.4), channel_id=1, source_target_pairs={{0,4},{4,8},{8,12},{12,16},{16,20},{20,24},{24,28},{1,5},{5,9},{9,... | collective-permute-start | bytes 393224 | tf_op jit(solution)/shard_map/ppermute | solution.py:12
  93.0 7.9 %collective-permute-start.6 = (bf16[128,512]{1,0:T(8,128)(2,1)}, bf16[128,512]{1,0:T(8,128)(2,1)}, u32[]{:S(2)}, u32[]{:S(2)}) collective-permute-start(bf16[128,512]{1,0:T(8,128)(2,1)} %collective-permute-done.5), channel_id=1, source_target_pairs={{0,4},{4,8},{8,12},{12,16},{16,20},{20,24},{24,28},{1,5},{5,9},{9,... | collective-permute-start | bytes 393224 | tf_op jit(solution)/shard_map/ppermute | solution.py:12
Sparse Core Ops, SparseCore 0:
  104.7 27.4 reduce-scatter.1
where the time goes:
time: 141 us
  waiting for transfers between devices  36.1 us (26%)
  starting transfers between devices  33.2 us (24%)
  local copies, waits for them, and re-layouts  25.4 us (18%)
  blocking collectives  19 us (13%)
  between operations  13.8 us (10%)
  matrix products  9.44 us (7%)
  other arithmetic  3.91 us (3%)
    ppermute x7, starting transfers between devices, shifted(): return lax.ppermute(array, axis, pairs)  33.1 us
    reduce_scatter x1, waiting for transfers between devices, on_device(): lax.psum_scatter(jnp.dot(mixed_out, out_weight, preferred_element_type=jn...  27.6 us
    all_gather x1, blocking collectives, on_device(): filters = lax.all_gather(long_filter, 'seq', axis=1, tiled=True)  19 us
    ppermute x6, local copies, waits for them, and re-layouts, shifted(): return lax.ppermute(array, axis, pairs)  9.33 us
    ppermute x7, waiting for transfers between devices, shifted(): return lax.ppermute(array, axis, pairs)  8.4 us
    rev x7, local copies, waits for them, and re-layouts, toeplitz_block(): return tiled_rows[:, :, :row_count][:, :, ::-1]  8.29 us
    dot_general x7, matrix products, add_offset(): jnp.einsum('gij,jgc->igc', matrix, shaped_block, preferred_element_type=j...  8.02 us
    another operation x14, local copies, waits for them, and re-layouts, toeplitz_block(): jnp.tile(window, (1, row_count + 1))[:, :2 * row_count * row_count]  3.87 us
  transfers between devices with their start and end apart: 8, of which 7 were waited for; matrix products, arithmetic and copies ran while one was open for 15% of the time, Pallas kernels for 0%

commit v1 on v0

--- a/solution.py
+++ b/solution.py
@@ -1,9 +1,14 @@
+import functools
+
 import jax
 import jax.numpy as jnp
 from jax import lax
+from jax.experimental import pallas as pl
+from jax.experimental.pallas import tpu as pltpu
 from jax.sharding import PartitionSpec as P
 
 REACH = 6
+EXTRA = 16
 
 
 def shifted(array, axis, by):
@@ -22,7 +27,7 @@
     return tiled_rows[:, :, :row_count][:, :, ::-1]
 
 
-def on_device(projected, short_filter, long_filter, out_weight):
+def ring_form(projected, short_filter, long_filter, out_weight):
     row_count, _, chan_count = projected.shape
     tap_count = short_filter.shape[-1]
     group_count = short_filter.shape[1]
@@ -65,6 +70,216 @@
     return result.astype(jnp.bfloat16)
 
 
+def lagged(stream, lag):
+    moved = pltpu.roll(stream, lag, axis=0)
+    rows = lax.broadcasted_iota(jnp.int32, stream.shape, 0)
+    return jnp.where(rows >= lag, moved, 0.0)
+
+
+def gate_kernel(copies, proj_ref, short_ref, long_ref, out_ref, extra_ref):
+    _, row_count, _ = proj_ref.shape
+    group_count = short_ref.shape[1]
+    width = proj_ref.shape[2] // group_count
+    lags = long_ref.shape[1]
+    taps = [short_ref[s].astype(jnp.float32) for s in range(3)]
+    long_rows = long_ref[...].astype(jnp.float32)
+    extra_ref[...] = jnp.zeros_like(extra_ref)
+    for g in range(group_count):
+        lanes = slice(g * width, (g + 1) * width)
+        raw = [proj_ref[s, :, lanes].astype(jnp.float32) for s in range(3)]
+        made = []
+        for s in (1, 2):
+            tap = [taps[s][g : g + 1, m : m + 1] for m in range(3)]
+            made.append(
+                tap[0] * raw[s] + tap[1] * lagged(raw[s], 1) + tap[2] * lagged(raw[s], 2)
+            )
+        gated = (made[0] * made[1]).astype(jnp.bfloat16)
+        extra_ref[g, 0:1, 0:lags] = long_rows[g : g + 1]
+        extra_ref[g, 1:3] = raw[1][0:2]
+        extra_ref[g, 3:5] = raw[2][0:2]
+        extra_ref[g, 5:7] = raw[1][row_count - 2 :]
+        extra_ref[g, 7:9] = raw[2][row_count - 2 :]
+        extra_ref[g, 9:11] = raw[0][row_count - 2 :]
+        extra = extra_ref[g].astype(jnp.bfloat16)
+        for x in range(copies):
+            out_ref[g * copies + x, 0:row_count] = gated
+            out_ref[g * copies + x, row_count:] = extra
+
+
+def filter_kernel(copies, lags, place_ref, in_ref, short_ref, out_ref, gated_ref):
+    seq_count, rows_sent, width = in_ref.shape
+    row_count = rows_sent - EXTRA
+    depth = REACH * row_count
+    me = place_ref[0]
+    group, part = me // copies, me % copies
+
+    picked = []
+    for s in (1, 2):
+        table = short_ref[s].astype(jnp.float32)
+        rows = lax.broadcasted_iota(jnp.int32, table.shape, 0)
+        row = jnp.sum(jnp.where(rows == group, table, 0.0), axis=0, keepdims=True)
+        picked.append([row[:, m : m + 1] for m in range(3)])
+
+    gated_ref[0:depth] = jnp.zeros((depth, width), jnp.bfloat16)
+    tile_rows = lax.broadcasted_iota(jnp.int32, (16, width), 0)
+    before = jnp.zeros((EXTRA, width), jnp.float32)
+    lag_rows = []
+    for s in range(seq_count):
+        here = in_ref[s, row_count:].astype(jnp.float32)
+        lag_rows.append(here[0:1])
+        heads = []
+        for stream in range(2):
+            tap = picked[stream]
+            first, second = here[1 + 2 * stream : 2 + 2 * stream], here[2 + 2 * stream : 3 + 2 * stream]
+            older, newer = before[5 + 2 * stream : 6 + 2 * stream], before[6 + 2 * stream : 7 + 2 * stream]
+            heads.append(
+                (
+                    tap[0] * first + tap[1] * newer + tap[2] * older,
+                    tap[0] * second + tap[1] * first + tap[2] * newer,
+                )
+            )
+        tile = in_ref[s, 0:16].astype(jnp.float32)
+        tile = jnp.where(tile_rows == 0, heads[0][0] * heads[1][0], tile)
+        tile = jnp.where(tile_rows == 1, heads[0][1] * heads[1][1], tile)
+        base = depth + s * row_count
+        gated_ref[base : base + 16] = tile.astype(jnp.bfloat16)
+        gated_ref[base + 16 : base + row_count] = in_ref[s, 16:row_count]
+        before = here
+
+    lags_back = jnp.concatenate(lag_rows[::-1], axis=0).astype(jnp.bfloat16)
+    i = lax.broadcasted_iota(jnp.int32, (width, width), 0)
+    k = lax.broadcasted_iota(jnp.int32, (width, width), 1)
+    flip = jnp.where(i + k == lags - 1, 1.0, 0.0).astype(jnp.bfloat16)
+    turned = jnp.dot(lags_back, flip, preferred_element_type=jnp.float32)
+    span = depth + 2 * row_count
+    first_lane = depth - lags * seq_count + 1
+    blank = jnp.zeros((1, span - width), jnp.float32)
+    line = jnp.zeros((1, span), jnp.float32)
+    for s in range(seq_count):
+        piece = jnp.concatenate([turned[s : s + 1], blank], axis=1)
+        line = line + pltpu.roll(piece, first_lane + lags * s, axis=1)
+    strip = pltpu.roll(
+        jnp.broadcast_to(line, (row_count, span)), 0, axis=1, stride=1, stride_axis=0
+    )
+    strip = strip[:, : depth + row_count].astype(jnp.bfloat16)
+
+    for z in range(out_ref.shape[0]):
+        block = z * copies + part
+        start = pl.multiple_of(block * row_count, row_count)
+        source = gated_ref[pl.ds(start, depth + row_count), :]
+        made = jnp.dot(strip, source, preferred_element_type=jnp.float32)
+        out_ref[z, 0:row_count] = made.astype(jnp.bfloat16)
+        rim = in_ref[jnp.maximum(block - 1, 0), row_count:].astype(jnp.float32)
+        out_ref[z, row_count:] = jnp.where(block > 0, rim, 0.0).astype(jnp.bfloat16)
+
+
+def project_kernel(place_ref, in_ref, proj_ref, short_ref, weight_ref, send_ref, keep_ref, mixed_ref):
+    group_count, rows_sent, width = in_ref.shape
+    row_count = rows_sent - EXTRA
+    taps = short_ref[0].astype(jnp.float32)
+    rows = lax.broadcasted_iota(jnp.int32, (row_count, width), 0)
+    for g in range(group_count):
+        lanes = slice(g * width, (g + 1) * width)
+        query = proj_ref[0, :, lanes].astype(jnp.float32)
+        rim = in_ref[g, row_count:].astype(jnp.float32)
+        older, newer = rim[9:10], rim[10:11]
+        one = jnp.where(rows == 0, newer, pltpu.roll(query, 1, axis=0))
+        two = jnp.where(rows == 0, older, jnp.where(rows == 1, newer, pltpu.roll(query, 2, axis=0)))
+        tap = [taps[g : g + 1, m : m + 1] for m in range(3)]
+        made = tap[0] * query + tap[1] * one + tap[2] * two
+        long_out = in_ref[g, 0:row_count].astype(jnp.float32)
+        mixed_ref[:, lanes] = (made * long_out).astype(jnp.bfloat16)
+    quarter = row_count // 4
+    me = place_ref[0]
+
+    def take(member):
+        return mixed_ref[pl.ds(pl.multiple_of(member * quarter, quarter), quarter), :]
+
+    ordered = jnp.concatenate([take(me ^ 1), take(me ^ 3), take(me), take(me ^ 2)], axis=0)
+    step = 512
+    for c in range(0, weight_ref.shape[1], step):
+        made = jnp.dot(
+            ordered, weight_ref[:, c : c + step], preferred_element_type=jnp.float32
+        )
+        send_ref[:, c : c + step] = made[: 2 * quarter].astype(jnp.bfloat16)
+        keep_ref[:, c : c + step] = made[2 * quarter :]
+
+
+def whole(space=pltpu.VMEM):
+    return pl.BlockSpec(memory_space=space)
+
+
+def exchange_form(projected, short_filter, long_filter, out_weight):
+    row_count, _, chan_count = projected.shape
+    group_count = short_filter.shape[1]
+    width = chan_count // group_count
+    seq_count = lax.axis_size("seq")
+    copies = seq_count // group_count
+    lags = long_filter.shape[1]
+    rows_sent = row_count + EXTRA
+    streams = jnp.transpose(projected, (1, 0, 2))
+    seq_place = lax.axis_index("seq").astype(jnp.int32).reshape(1)
+    chan_place = lax.axis_index("chan").astype(jnp.int32).reshape(1)
+
+    outgoing = pl.pallas_call(
+        functools.partial(gate_kernel, copies),
+        out_shape=jax.ShapeDtypeStruct((seq_count, rows_sent, width), jnp.bfloat16),
+        in_specs=[whole()] * 3,
+        out_specs=whole(),
+        scratch_shapes=[pltpu.VMEM((group_count, EXTRA, width), jnp.float32)],
+        name="gate",
+    )(streams, short_filter, long_filter)
+    arrived = lax.all_to_all(outgoing, "seq", 0, 0)
+    made = pl.pallas_call(
+        functools.partial(filter_kernel, copies, lags),
+        out_shape=jax.ShapeDtypeStruct((group_count, rows_sent, width), jnp.bfloat16),
+        in_specs=[whole(pltpu.SMEM), whole(), whole()],
+        out_specs=whole(),
+        scratch_shapes=[pltpu.VMEM(((REACH + seq_count) * row_count, width), jnp.bfloat16)],
+        name="long_filter",
+    )(seq_place, arrived, short_filter)
+    same_part = [[z * copies + x for z in range(group_count)] for x in range(copies)]
+    returned = lax.all_to_all(made, "seq", 0, 0, axis_index_groups=same_part)
+    half = row_count // 2
+    send, keep = pl.pallas_call(
+        project_kernel,
+        out_shape=(
+            jax.ShapeDtypeStruct((half, out_weight.shape[1]), jnp.bfloat16),
+            jax.ShapeDtypeStruct((half, out_weight.shape[1]), jnp.float32),
+        ),
+        in_specs=[whole(pltpu.SMEM)] + [whole()] * 4,
+        out_specs=(whole(), whole()),
+        scratch_shapes=[pltpu.VMEM((row_count, chan_count), jnp.bfloat16)],
+        name="project",
+    )(chan_place, returned, streams, short_filter, out_weight)
+    near = lax.ppermute(send, "chan", [(c, c ^ 1) for c in range(4)])
+    quarter = half // 2
+    onward = (keep[quarter:] + near[quarter:].astype(jnp.float32)).astype(jnp.bfloat16)
+    far = lax.ppermute(onward, "chan", [(c, c ^ 2) for c in range(4)])
+    mine = keep[:quarter] + near[:quarter].astype(jnp.float32)
+    return (mine + far.astype(jnp.float32)).astype(jnp.bfloat16)
+
+
+def on_device(projected, short_filter, long_filter, out_weight):
+    row_count, _, chan_count = projected.shape
+    group_count = short_filter.shape[1]
+    width = chan_count // group_count
+    seq_count = lax.axis_size("seq")
+    exchanged = (seq_count + group_count) * (row_count + EXTRA) * width
+    ringed = REACH * row_count * chan_count
+    fits = (
+        seq_count % group_count == 0
+        and seq_count * long_filter.shape[1] <= REACH * row_count
+        and long_filter.shape[1] <= width
+        and width == 128
+        and row_count % 64 == 0
+        and short_filter.shape[-1] == 3
+        and lax.axis_size("chan") == 4
+    )
+    form = exchange_form if fits and exchanged < ringed else ring_form
+    return form(projected, short_filter, long_filter, out_weight)
+
+
 def solution(mesh):
     return jax.shard_map(
         on_device,

time: 141 us -> 45.6 us (0.32)
  local copies, waits for them, and re-layouts: 25.4 us -> 1.38 us
  starting transfers between devices: 33.2 us -> 12.2 us
  blocking collectives: 19 us -> 0 us
  waiting for transfers between devices: 36.1 us -> 21.3 us
  between operations: 13.8 us -> 0.02 us
  matrix products: 9.44 us -> 0 us
  Pallas kernels: 0 us -> 7.63 us
    ppermute x7 -> x2, starting transfers between devices: 33.1 us -> 1.58 us  [the longest x1 1.58 us: exchange_form(): far = lax.ppermute(onward, 'chan', [(c, c ^ 2) for c in range(4)])]
    reduce_scatter x1 -> x0, waiting for transfers between devices: 27.6 us -> none  [on_device(): lax.psum_scatter(jnp.dot(mixed_out, out_weight, preferred_element_type=jn...]
    all_gather x1 -> x0, blocking collectives: 19 us -> none  [on_device(): filters = lax.all_gather(long_filter, 'seq', axis=1, tiled=True)]
    all_to_all x0 -> x2, waiting for transfers between devices: none -> 15.5 us  [the longest x1 9.61 us: exchange_form(): arrived = lax.all_to_all(outgoing, 'seq', 0, 0)]
    all_to_all x0 -> x2, starting transfers between devices: none -> 10.6 us  [the longest x1 7.28 us: exchange_form(): arrived = lax.all_to_all(outgoing, 'seq', 0, 0)]
    dot_general x8 -> x0, matrix products: 9.44 us -> none  [the longest x7 8.02 us: add_offset(): jnp.einsum('gij,jgc->igc', matrix, shaped_block, preferred_element_type=j...]
    ppermute x6 -> x0, local copies, waits for them, and re-layouts: 9.33 us -> none  [shifted(): return lax.ppermute(array, axis, pairs)]
    rev x7 -> x0, local copies, waits for them, and re-layouts: 8.29 us -> none  [toeplitz_block(): return tiled_rows[:, :, :row_count][:, :, ::-1]]
  transfers between devices with their start and end apart: 8 -> 4, of which waited for: 7 -> 4; matrix products, arithmetic and copies ran while one was open for 15% -> 0% of each run, Pallas kernels for 0% -> 0%
where the time goes in v1:
time: 45.6 us; the launch traced here: 45.2 us
  waiting for transfers between devices  21.3 us (47%)
  starting transfers between devices  12.2 us (27%)
  Pallas kernels  7.63 us (17%)
  other arithmetic  2.63 us (6%)
  local copies, waits for them, and re-layouts  1.38 us (3%)
    all_to_all x1, waiting for transfers between devices, exchange_form(): arrived = lax.all_to_all(outgoing, 'seq', 0, 0)  9.61 us
    all_to_all x1, starting transfers between devices, exchange_form(): arrived = lax.all_to_all(outgoing, 'seq', 0, 0)  7.28 us
    all_to_all x1, waiting for transfers between devices, exchange_form(): returned = lax.all_to_all(made, 'seq', 0, 0, axis_index_groups=same_part)  5.93 us
    ppermute x1, waiting for transfers between devices, exchange_form(): far = lax.ppermute(onward, 'chan', [(c, c ^ 2) for c in range(4)])  4.02 us
    all_to_all x1, starting transfers between devices, exchange_form(): returned = lax.all_to_all(made, 'seq', 0, 0, axis_index_groups=same_part)  3.33 us
    pallas_call x1, Pallas kernels, exchange_form(): pl.pallas_call(project_kernel, out_shape=(jax.ShapeDtypeStruct((half, out...  3.3 us
    pallas_call x1, Pallas kernels, exchange_form(): pl.pallas_call(functools.partial(filter_kernel, copies, lags), out_shape=...  2.34 us
    pallas_call x1, Pallas kernels, exchange_form(): pl.pallas_call(functools.partial(gate_kernel, copies), out_shape=jax.Shap...  1.99 us
  transfers between devices with their start and end apart: 4, of which 4 were waited for; matrix products, arithmetic and copies ran while one was open for 0% of the time, Pallas kernels for 0%

profile of v1, /device:TPU:0, one launch (start us, length us, event | category | flops | bytes accessed | tf_op | source)
XLA Modules:
  0.0 45.2 jit_solution(4696839625457869010)
XLA Ops:
  0.0 2.0 %gate.1 = bf16[8,144,128]{2,1,0:T(8,128)(2,1)} custom-call(bf16[3,128,512]{2,1,0:T(8,128)(2,1)} %bitcast.3, bf16[3,4,3]{2,1,0:T(4,128)(2,1)} %short_ref.5, bf16[4,96]{1,0:T(4,128)(2,1)} %long_ref.1), custom_call_target="tpu_custom_call" | custom-call | tf_op jit(solution)/shard_map/gate/pallas_call | solution.py:224
  2.0 7.3 %all-to-all-start = ((bf16[8,144,128]{2,1,0:T(8,128)(2,1)}), bf16[8,144,128]{2,1,0:T(8,128)(2,1)S(1)}, u32[]{:S(2)}, u32[]{:S(2)}) async-start(bf16[8,144,128]{2,1,0:T(8,128)(2,1)} %gate.1), calls=%async_computation | async-start | bytes 589824 | tf_op jit(solution)/shard_map/all_to_all | solution.py:232
  9.3 9.6 %all-to-all-done.in_ref = bf16[8,144,128]{2,1,0:T(8,128)(2,1)S(1)} async-done(((bf16[8,144,128]{2,1,0:T(8,128)(2,1)}), bf16[8,144,128]{2,1,0:T(8,128)(2,1)S(1)}, u32[]{:S(2)}, u32[]{:S(2)}) %all-to-all-start) | async-done | bytes 294944 | tf_op jit(solution)/shard_map/all_to_all | solution.py:232
  18.9 0.0 copy-start
  18.9 0.7 %copy-done = bf16[8,144,128]{2,1,0:T(8,128)(2,1)} copy-done((bf16[8,144,128]{2,1,0:T(8,128)(2,1)}, bf16[8,144,128]{2,1,0:T(8,128)(2,1)S(1)}, u32[]{:S(2)}) %copy-start) | copy-done | bytes 294936
  19.6 2.3 %long_filter.1 = bf16[4,144,128]{2,1,0:T(8,128)(2,1)} custom-call(s32[1]{0:T(128)} %bitcast.1.place_ref, bf16[8,144,128]{2,1,0:T(8,128)(2,1)} %copy-done, bf16[3,4,3]{2,1,0:T(4,128)(2,1)} %short_ref.5), custom_call_target="tpu_custom_call" | custom-call | tf_op jit(solution)/shard_map/long_filter/pallas_call | solution.py:233
  21.9 3.3 %all-to-all-start.1 = ((bf16[4,144,128]{2,1,0:T(8,128)(2,1)}), bf16[4,144,128]{2,1,0:T(8,128)(2,1)S(1)}, u32[]{:S(2)}, u32[]{:S(2)}) async-start(bf16[4,144,128]{2,1,0:T(8,128)(2,1)} %long_filter.1), calls=%async_computation.1 | async-start | bytes 294912 | tf_op jit(solution)/shard_map/all_to_all | solution.py:242
  25.3 5.9 %all-to-all-done.1.in_ref = bf16[4,144,128]{2,1,0:T(8,128)(2,1)S(1)} async-done(((bf16[4,144,128]{2,1,0:T(8,128)(2,1)}), bf16[4,144,128]{2,1,0:T(8,128)(2,1)S(1)}, u32[]{:S(2)}, u32[]{:S(2)}) %all-to-all-start.1) | async-done | bytes 147488 | tf_op jit(solution)/shard_map/all_to_all | solution.py:242
  31.2 0.0 copy-start.1
  31.2 0.7 %copy-done.1 = bf16[4,144,128]{2,1,0:T(8,128)(2,1)} copy-done((bf16[4,144,128]{2,1,0:T(8,128)(2,1)}, bf16[4,144,128]{2,1,0:T(8,128)(2,1)S(1)}, u32[]{:S(2)}) %copy-start.1) | copy-done | bytes 147480
  31.9 3.3 %project.1 = (bf16[64,2048]{1,0:T(8,128)(2,1)}, f32[64,2048]{1,0:T(8,128)}) custom-call(s32[1]{0:T(128)} %bitcast.place_ref, bf16[4,144,128]{2,1,0:T(8,128)(2,1)} %copy-done.1, bf16[3,128,512]{2,1,0:T(8,128)(2,1)} %bitcast.4, bf16[3,4,3]{2,1,0:T(4,128)(2,1)} %short_ref.5, bf16[512,2048]{1,0:T(8,128)(2,1)} %weight_ref.1), custom_call_target="tpu_custom_call" | custom-call | tf_op jit(solution)/shard_map/project/pallas_call | solution.py:244
  35.2 0.0 collective-permute-start
  35.2 1.7 %collective-permute-done = bf16[64,2048]{1,0:T(8,128)(2,1)S(1)} collective-permute-done((bf16[64,2048]{1,0:T(8,128)(2,1)}, bf16[64,2048]{1,0:T(8,128)(2,1)S(1)}, u32[]{:S(2)}, u32[]{:S(2)}) %collective-permute-start) | collective-permute-done | bytes 262176 | tf_op jit(solution)/shard_map/ppermute | solution.py:255
  36.9 1.0 %add_convert_fusion.1 = bf16[32,2048]{1,0:T(8,128)(2,1)S(1)} fusion(f32[64,2048]{1,0:T(8,128)} %get-tuple-element.7, bf16[64,2048]{1,0:T(8,128)(2,1)S(1)} %collective-permute-done), kind=kLoop, calls=%fused_computation.1 | loop fusion | flops 196608 | bytes 524288 | tf_op jit(solution)/shard_map/convert_element_type | solution.py:257
  37.9 1.6 %collective-permute-start.1 = (bf16[32,2048]{1,0:T(8,128)(2,1)S(1)}, bf16[32,2048]{1,0:T(8,128)(2,1)S(1)}, u32[]{:S(2)}, u32[]{:S(2)}) collective-permute-start(bf16[32,2048]{1,0:T(8,128)(2,1)S(1)} %add_convert_fusion.1), channel_id=1, source_target_pairs={{0,2},{1,3},{2,0},{3,1},{4,6},{5,7},{6,4},{7,5},{8,10},{9,11},{10,... | collective-permute-start | bytes 393224 | tf_op jit(solution)/shard_map/ppermute | solution.py:258
  39.5 4.0 %collective-permute-done.1 = bf16[32,2048]{1,0:T(8,128)(2,1)S(1)} collective-permute-done((bf16[32,2048]{1,0:T(8,128)(2,1)S(1)}, bf16[32,2048]{1,0:T(8,128)(2,1)S(1)}, u32[]{:S(2)}, u32[]{:S(2)}) %collective-permute-start.1) | collective-permute-done | bytes 131104 | tf_op jit(solution)/shard_map/ppermute | solution.py:258
  43.5 1.7 %add_convert_fusion = bf16[32,2048]{1,0:T(8,128)(2,1)} fusion(bf16[32,2048]{1,0:T(8,128)(2,1)S(1)} %collective-permute-done.1, f32[64,2048]{1,0:T(8,128)} %get-tuple-element.7, bf16[64,2048]{1,0:T(8,128)(2,1)S(1)} %collective-permute-done), kind=kLoop, calls=%fused_computation | loop fusion | flops 327680 | bytes 655360 | tf_op jit(solution)/shard_map/convert_element_type | solution.py:260
Async XLA Ops:
  2.0 16.9 %all-to-all-start = ((bf16[8,144,128]{2,1,0:T(8,128)(2,1)}), bf16[8,144,128]{2,1,0:T(8,128)(2,1)S(1)}, u32[]{:S(2)}, u32[]{:S(2)}) async-start(bf16[8,144,128]{2,1,0:T(8,128)(2,1)} %gate.1), calls=%async_computation | async-start | bytes 589824 | tf_op jit(solution)/shard_map/all_to_all | solution.py:232
  18.9 0.7 %copy-start = (bf16[8,144,128]{2,1,0:T(8,128)(2,1)}, bf16[8,144,128]{2,1,0:T(8,128)(2,1)S(1)}, u32[]{:S(2)}) copy-start(bf16[8,144,128]{2,1,0:T(8,128)(2,1)S(1)} %all-to-all-done.in_ref) | copy-start | bytes 884740
  21.9 9.3 %all-to-all-start.1 = ((bf16[4,144,128]{2,1,0:T(8,128)(2,1)}), bf16[4,144,128]{2,1,0:T(8,128)(2,1)S(1)}, u32[]{:S(2)}, u32[]{:S(2)}) async-start(bf16[4,144,128]{2,1,0:T(8,128)(2,1)} %long_filter.1), calls=%async_computation.1 | async-start | bytes 294912 | tf_op jit(solution)/shard_map/all_to_all | solution.py:242
  31.2 0.7 %copy-start.1 = (bf16[4,144,128]{2,1,0:T(8,128)(2,1)}, bf16[4,144,128]{2,1,0:T(8,128)(2,1)S(1)}, u32[]{:S(2)}) copy-start(bf16[4,144,128]{2,1,0:T(8,128)(2,1)S(1)} %all-to-all-done.1.in_ref) | copy-start | bytes 442372
  35.2 1.7 %collective-permute-start = (bf16[64,2048]{1,0:T(8,128)(2,1)}, bf16[64,2048]{1,0:T(8,128)(2,1)S(1)}, u32[]{:S(2)}, u32[]{:S(2)}) collective-permute-start(bf16[64,2048]{1,0:T(8,128)(2,1)} %get-tuple-element.8), channel_id=1, source_target_pairs={{0,1},{1,0},{2,3},{3,2},{4,5},{5,4},{6,7},{7,6},{8,9},{9,8},{10,11... | collective-permute-start | bytes 786440 | tf_op jit(solution)/shard_map/ppermute | solution.py:255
  37.9 5.6 %collective-permute-start.1 = (bf16[32,2048]{1,0:T(8,128)(2,1)S(1)}, bf16[32,2048]{1,0:T(8,128)(2,1)S(1)}, u32[]{:S(2)}, u32[]{:S(2)}) collective-permute-start(bf16[32,2048]{1,0:T(8,128)(2,1)S(1)} %add_convert_fusion.1), channel_id=1, source_target_pairs={{0,2},{1,3},{2,0},{3,1},{4,6},{5,7},{6,4},{7,5},{8,10},{9,11},{10,... | collective-permute-start | bytes 393224 | tf_op jit(solution)/shard_map/ppermute | solution.py:258

commit v2 on v1

v2 whole, which is shorter than its diff:
```python
import functools

import jax
import jax.numpy as jnp
from jax import lax
from jax.experimental import pallas as pl
from jax.experimental.pallas import tpu as pltpu
from jax.sharding import PartitionSpec as P

REACH = 6
EXTRA = 8


def shifted(array, axis, by):
    peers = lax.axis_size(axis)
    pairs = [(i, i + by) for i in range(peers) if 0 <= i + by < peers]
    return lax.ppermute(array, axis, pairs)


def toeplitz_block(padded, offset, row_count):
    group_count = padded.shape[0]
    window = lax.slice_in_dim(
        padded, offset * row_count + 1, offset * row_count + 2 * row_count, axis=1
    )
    tiled_rows = jnp.tile(window, (1, row_count + 1))[:, : 2 * row_count * row_count]
    tiled_rows = tiled_rows.reshape(group_count, row_count, 2 * row_count)
    return tiled_rows[:, :, :row_count][:, :, ::-1]


def ring_form(projected, short_filter, long_filter, out_weight):
    row_count, _, chan_count = projected.shape
    tap_count = short_filter.shape[-1]
    group_count = short_filter.shape[1]
    group_width = chan_count // group_count
    tail_rows = projected[row_count - tap_count + 1 :]
    arrived_rim = shifted(tail_rows, "seq", 1)
    padded_rows = jnp.concatenate([arrived_rim, projected], axis=0)
    channel_taps = jnp.repeat(short_filter.astype(jnp.float32), group_width, axis=1)
    streams = jnp.zeros((row_count, 3, chan_count), jnp.float32)
    for lag in range(tap_count):
        begin = tap_count - 1 - lag
        window = lax.slice_in_dim(padded_rows, begin, begin + row_count, axis=0)
        streams = streams + channel_taps[None, :, :, lag] * window.astype(jnp.float32)
    query_part = streams[:, 0]
    gated_input = (streams[:, 1] * streams[:, 2]).astype(jnp.bfloat16)
    filters = lax.all_gather(long_filter, "seq", axis=1, tiled=True)
    padded = jnp.pad(filters, ((0, 0), (row_count, row_count)))

    def add_offset(running, offset, source_block):
        matrix = toeplitz_block(padded, offset, row_count)
        shaped_block = source_block.reshape(row_count, group_count, group_width)
        return running + jnp.einsum(
            "gij,jgc->igc", matrix, shaped_block, preferred_element_type=jnp.float32
        )

    running = add_offset(
        jnp.zeros((row_count, group_count, group_width), jnp.float32), 0, gated_input
    )
    moving = gated_input
    for offset in range(1, REACH + 1):
        moving = shifted(moving, "seq", 1)
        running = add_offset(running, offset, moving)
    mixed_out = (query_part * running.reshape(row_count, chan_count)).astype(jnp.bfloat16)
    result = lax.psum_scatter(
        jnp.dot(mixed_out, out_weight, preferred_element_type=jnp.float32),
        "chan",
        scatter_dimension=0,
        tiled=True,
    )
    return result.astype(jnp.bfloat16)


def lagged(stream, lag):
    moved = pltpu.roll(stream, lag, axis=0)
    rows = lax.broadcasted_iota(jnp.int32, stream.shape, 0)
    return jnp.where(rows >= lag, moved, 0.0)


def short_sum(stream, table, group):
    tap = [table[group : group + 1, m : m + 1] for m in range(3)]
    return tap[0] * stream + tap[1] * lagged(stream, 1) + tap[2] * lagged(stream, 2)


def gate_kernel(copies, proj_hbm, short_hbm, long_hbm, out_hbm, proj_ref, short_ref, long_ref, extra_ref, made_ref, sems, out_sems):
    group_count, _, row_count, width = proj_ref.shape
    lags = long_ref.shape[1]
    small = [
        pltpu.make_async_copy(short_hbm, short_ref, sems.at[0]),
        pltpu.make_async_copy(long_hbm, long_ref, sems.at[1]),
    ]
    large = [
        pltpu.make_async_copy(
            proj_hbm.at[1:3, :, g * width : (g + 1) * width], proj_ref.at[g], sems.at[2 + g]
        )
        for g in range(group_count)
    ]
    for copy in small + large:
        copy.start()
    extra_ref[...] = jnp.zeros_like(extra_ref)
    for copy in small:
        copy.wait()
    tables = [short_ref[s].astype(jnp.float32) for s in (1, 2)]
    long_rows = long_ref[...].astype(jnp.float32)
    leaving = []
    for g in range(group_count):
        large[g].wait()
        key, value = (proj_ref[g, s].astype(jnp.float32) for s in range(2))
        gated = short_sum(key, tables[0], g) * short_sum(value, tables[1], g)
        rows = lax.broadcasted_iota(jnp.int32, gated.shape, 0)
        extra_ref[g, 0:1, 0:lags] = long_rows[g : g + 1]
        extra_ref[g, 1:3] = value[0:2]
        extra_ref[g, 3:5] = key[row_count - 2 :]
        extra_ref[g, 5:7] = value[row_count - 2 :]
        made_ref[g, 0:row_count] = jnp.where(rows < 2, key, gated).astype(jnp.bfloat16)
        made_ref[g, row_count:] = extra_ref[g].astype(jnp.bfloat16)
        for x in range(copies):
            member = g * copies + x
            copy = pltpu.make_async_copy(made_ref.at[g], out_hbm.at[member], out_sems.at[member])
            copy.start()
            leaving.append(copy)
    for copy in leaving:
        copy.wait()


def ready_kernel(proj_hbm, short_hbm, weight_hbm, query_ref, table_ref, weight_ref, proj_ref, short_ref, sems):
    copies = [
        pltpu.make_async_copy(short_hbm, short_ref, sems.at[0]),
        pltpu.make_async_copy(proj_hbm.at[0], proj_ref, sems.at[1]),
        pltpu.make_async_copy(weight_hbm, weight_ref, sems.at[2]),
    ]
    for copy in copies:
        copy.start()
    copies[0].wait()
    for s in range(3):
        table_ref[s] = short_ref[s].astype(jnp.float32)
    table = short_ref[0].astype(jnp.float32)
    group_count = table.shape[0]
    width = query_ref.shape[1] // group_count
    copies[1].wait()
    for g in range(group_count):
        lanes = slice(g * width, (g + 1) * width)
        query_ref[:, lanes] = short_sum(proj_ref[:, lanes].astype(jnp.float32), table, g)
    copies[2].wait()


def filter_kernel(copies, lags, place_ref, in_ref, table_ref, out_hbm, gated_ref, made_ref, sems):
    seq_count, rows_sent, width = in_ref.shape
    row_count = rows_sent - EXTRA
    depth = REACH * row_count
    me = place_ref[0]
    group, part = me // copies, me % copies

    extras = [in_ref[s, row_count:].astype(jnp.float32) for s in range(seq_count)]
    lags_back = jnp.concatenate([e[0:1] for e in extras[::-1]], axis=0).astype(jnp.bfloat16)
    i = lax.broadcasted_iota(jnp.int32, (width, width), 0)
    k = lax.broadcasted_iota(jnp.int32, (width, width), 1)
    flip = jnp.where(i + k == lags - 1, 1.0, 0.0).astype(jnp.bfloat16)
    turned = jnp.dot(lags_back, flip, preferred_element_type=jnp.float32)
    span = depth + 2 * row_count
    first_lane = depth - lags * seq_count + 1
    blank = jnp.zeros((1, span - width), jnp.float32)
    line = jnp.zeros((1, span), jnp.float32)
    for s in range(seq_count):
        piece = jnp.concatenate([turned[s : s + 1], blank], axis=1)
        line = line + pltpu.roll(piece, first_lane + lags * s, axis=1)
    strip = pltpu.roll(
        jnp.broadcast_to(line, (row_count, span)), 0, axis=1, stride=1, stride_axis=0
    )
    strip = strip[:, : depth + row_count].astype(jnp.bfloat16)

    picked = []
    for s in (1, 2):
        table = table_ref[s]
        rows = lax.broadcasted_iota(jnp.int32, table.shape, 0)
        row = jnp.sum(jnp.where(rows == group, table, 0.0), axis=0, keepdims=True)
        picked.append([row[:, m : m + 1] for m in range(3)])

    gated_ref[0:depth] = jnp.zeros((depth, width), jnp.bfloat16)
    tile_rows = lax.broadcasted_iota(jnp.int32, (16, width), 0)
    before = jnp.zeros((EXTRA, width), jnp.float32)
    for s in range(seq_count):
        here = extras[s]
        tile = in_ref[s, 0:16].astype(jnp.float32)
        heads = []
        for stream, head in enumerate((tile[0:2], here[1:3])):
            tap = picked[stream]
            first, second = head[0:1], head[1:2]
            older, newer = before[3 + 2 * stream : 4 + 2 * stream], before[4 + 2 * stream : 5 + 2 * stream]
            heads.append(
                (
                    tap[0] * first + tap[1] * newer + tap[2] * older,
                    tap[0] * second + tap[1] * first + tap[2] * newer,
                )
            )
        tile = jnp.where(tile_rows == 0, heads[0][0] * heads[1][0], tile)
        tile = jnp.where(tile_rows == 1, heads[0][1] * heads[1][1], tile)
        base = depth + s * row_count
        gated_ref[base : base + 16] = tile.astype(jnp.bfloat16)
        gated_ref[base + 16 : base + row_count] = in_ref[s, 16:row_count]
        before = here

    leaving = []
    for z in range(out_hbm.shape[0]):
        start = pl.multiple_of((z * copies + part) * row_count, row_count)
        source = gated_ref[pl.ds(start, depth + row_count), :]
        made = jnp.dot(strip, source, preferred_element_type=jnp.float32)
        made_ref[z] = made.astype(jnp.bfloat16)
        copy = pltpu.make_async_copy(made_ref.at[z], out_hbm.at[z], sems.at[z])
        copy.start()
        leaving.append(copy)
    for copy in leaving:
        copy.wait()


def project_kernel(place_ref, in_ref, query_ref, rim_ref, table_ref, weight_ref, send_ref, keep_ref, mixed_ref):
    group_count, row_count, width = in_ref.shape
    table = table_ref[0]
    rows = lax.broadcasted_iota(jnp.int32, (8, width), 0)
    rim = rim_ref[...].astype(jnp.float32)
    for g in range(group_count):
        lanes = slice(g * width, (g + 1) * width)
        older, newer = rim[0:1, lanes], rim[1:2, lanes]
        one, two = table[g : g + 1, 1:2], table[g : g + 1, 2:3]
        head = query_ref[0:8, lanes]
        head = head + jnp.where(rows == 0, one * newer + two * older, 0.0)
        head = head + jnp.where(rows == 1, two * newer, 0.0)
        query = jnp.concatenate([head, query_ref[8:, lanes]], axis=0)
        mixed_ref[:, lanes] = (query * in_ref[g].astype(jnp.float32)).astype(jnp.bfloat16)
    quarter = row_count // 4
    me = place_ref[0]

    def take(member):
        return mixed_ref[pl.ds(pl.multiple_of(member * quarter, quarter), quarter), :]

    ordered = jnp.concatenate([take(me ^ 1), take(me ^ 3), take(me), take(me ^ 2)], axis=0)
    step = 512
    for c in range(0, weight_ref.shape[1], step):
        made = jnp.dot(
            ordered, weight_ref[:, c : c + step], preferred_element_type=jnp.float32
        )
        send_ref[:, c : c + step] = made[: 2 * quarter].astype(jnp.bfloat16)
        keep_ref[:, c : c + step] = made[2 * quarter :]


def room(mib):
    return pltpu.CompilerParams(vmem_limit_bytes=mib << 20)


def cost(flops, moved):
    return pl.CostEstimate(flops=flops, bytes_accessed=moved, transcendentals=0)


def whole(space=pltpu.VMEM):
    return pl.BlockSpec(memory_space=space)


def exchange_form(projected, short_filter, long_filter, out_weight):
    row_count, _, chan_count = projected.shape
    group_count = short_filter.shape[1]
    width = chan_count // group_count
    out_count = out_weight.shape[1]
    seq_count = lax.axis_size("seq")
    copies = seq_count // group_count
    lags = long_filter.shape[1]
    rows_sent = row_count + EXTRA
    streams = jnp.transpose(projected, (1, 0, 2))
    seq_place = lax.axis_index("seq").astype(jnp.int32).reshape(1)
    chan_place = lax.axis_index("chan").astype(jnp.int32).reshape(1)
    block_bytes = row_count * chan_count * 2

    outgoing = pl.pallas_call(
        functools.partial(gate_kernel, copies),
        out_shape=jax.ShapeDtypeStruct((seq_count, rows_sent, width), jnp.bfloat16),
        in_specs=[whole(pltpu.HBM)] * 3,
        out_specs=whole(pltpu.HBM),
        scratch_shapes=[
            pltpu.VMEM((group_count, 2, row_count, width), projected.dtype),
            pltpu.VMEM(short_filter.shape, short_filter.dtype),
            pltpu.VMEM(long_filter.shape, long_filter.dtype),
            pltpu.VMEM((group_count, EXTRA, width), jnp.float32),
            pltpu.VMEM((group_count, rows_sent, width), jnp.bfloat16),
            pltpu.SemaphoreType.DMA((2 + group_count,)),
            pltpu.SemaphoreType.DMA((seq_count,)),
        ],
        cost_estimate=cost(12 * row_count * chan_count, 4 * block_bytes),
        name="gate",
    )(streams, short_filter, long_filter)
    arrived = lax.all_to_all(outgoing, "seq", 0, 0)

    query, table, weight = pl.pallas_call(
        ready_kernel,
        out_shape=(
            jax.ShapeDtypeStruct((row_count, chan_count), jnp.float32),
            jax.ShapeDtypeStruct(short_filter.shape, jnp.float32),
            jax.ShapeDtypeStruct(out_weight.shape, out_weight.dtype),
        ),
        in_specs=[whole(pltpu.HBM)] * 3,
        out_specs=(whole(), whole(), whole()),
        scratch_shapes=[
            pltpu.VMEM((row_count, chan_count), projected.dtype),
            pltpu.VMEM(short_filter.shape, short_filter.dtype),
            pltpu.SemaphoreType.DMA((3,)),
        ],
        compiler_params=room(4),
        cost_estimate=cost(6 * row_count * chan_count, 2 * chan_count * out_count + 3 * block_bytes),
        name="ready",
    )(streams, short_filter, out_weight)
    rim = shifted(projected[row_count - 2 :, 0], "seq", 1)

    made = pl.pallas_call(
        functools.partial(filter_kernel, copies, lags),
        out_shape=jax.ShapeDtypeStruct((group_count, row_count, width), jnp.bfloat16),
        in_specs=[whole(pltpu.SMEM), whole(), whole()],
        out_specs=whole(pltpu.HBM),
        scratch_shapes=[
            pltpu.VMEM(((REACH + seq_count) * row_count, width), jnp.bfloat16),
            pltpu.VMEM((group_count, row_count, width), jnp.bfloat16),
            pltpu.SemaphoreType.DMA((group_count,)),
        ],
        compiler_params=room(4),
        cost_estimate=cost(
            2 * group_count * (REACH + 1) * row_count * row_count * width, 4 * block_bytes
        ),
        name="long_filter",
    )(seq_place, arrived, table)
    same_part = [[z * copies + x for z in range(group_count)] for x in range(copies)]
    returned = lax.all_to_all(made, "seq", 0, 0, axis_index_groups=same_part)
    half = row_count // 2
    send, keep = pl.pallas_call(
        project_kernel,
        out_shape=(
            jax.ShapeDtypeStruct((half, out_count), jnp.bfloat16),
            jax.ShapeDtypeStruct((half, out_count), jnp.float32),
        ),
        in_specs=[whole(pltpu.SMEM)] + [whole()] * 5,
        out_specs=(whole(), whole()),
        scratch_shapes=[pltpu.VMEM((row_count, chan_count), jnp.bfloat16)],
        compiler_params=room(4),
        cost_estimate=cost(2 * row_count * chan_count * out_count, 2 * chan_count * out_count),
        name="project",
    )(chan_place, returned, query, rim, table, weight)
    near = lax.ppermute(send, "chan", [(c, c ^ 1) for c in range(4)])
    quarter = half // 2
    onward = (keep[quarter:] + near[quarter:].astype(jnp.float32)).astype(jnp.bfloat16)
    far = lax.ppermute(onward, "chan", [(c, c ^ 2) for c in range(4)])
    mine = keep[:quarter] + near[:quarter].astype(jnp.float32)
    return (mine + far.astype(jnp.float32)).astype(jnp.bfloat16)


def on_device(projected, short_filter, long_filter, out_weight):
    row_count, _, chan_count = projected.shape
    group_count = short_filter.shape[1]
    width = chan_count // group_count
    seq_count = lax.axis_size("seq")
    exchanged = (seq_count + group_count) * (row_count + EXTRA) * width
    ringed = REACH * row_count * chan_count
    fits = (
        seq_count % group_count == 0
        and seq_count * long_filter.shape[1] <= REACH * row_count
        and long_filter.shape[1] <= width
        and width == 128
        and row_count % 64 == 0
        and short_filter.shape[-1] == 3
        and lax.axis_size("chan") == 4
    )
    form = exchange_form if fits and exchanged < ringed else ring_form
    return form(projected, short_filter, long_filter, out_weight)


def solution(mesh):
    return jax.shard_map(
        on_device,
        mesh=mesh,
        in_specs=(P("seq", None, "chan"), P(None, "chan", None), P("chan", "seq"), P("chan", None)),
        out_specs=P(("seq", "chan"), None),
        check_vma=False,
    )
```

time: 45.6 us -> 38.4 us (0.84)
  waiting for transfers between devices: 21.3 us -> 12.9 us
  starting transfers between devices: 12.2 us -> 15.6 us
  Pallas kernels: 7.63 us -> 4.48 us
  local copies, waits for them, and re-layouts: 1.38 us -> 3.97 us
  other arithmetic: 2.63 us -> 0.73 us
    all_to_all x1, waiting for transfers between devices: 5.93 us -> 0.57 us  [exchange_form(): returned = lax.all_to_all(made, 'seq', 0, 0, axis_index_groups=same_part)]
    all_to_all x1, waiting for transfers between devices: 9.61 us -> 5.5 us  [exchange_form(): arrived = lax.all_to_all(outgoing, 'seq', 0, 0)]
    ppermute x0 -> x1, starting transfers between devices: none -> 3.31 us  [shifted(): return lax.ppermute(array, axis, pairs)]
    pallas_call x1, Pallas kernels: 3.3 us -> 0.49 us  [exchange_form(): pl.pallas_call(project_kernel, out_shape=(jax.ShapeDtypeStruct((half, out...]
    unnamed x4 -> x6, local copies, waits for them, and re-layouts: 1.38 us -> 3.27 us
    ppermute x0 -> x1, waiting for transfers between devices: none -> 1.29 us  [shifted(): return lax.ppermute(array, axis, pairs)]
    pallas_call x1, Pallas kernels: 2.34 us -> 1.38 us  [exchange_form(): pl.pallas_call(functools.partial(filter_kernel, copies, lags), out_shape=...]
    convert_element_type x1, other arithmetic: 0.98 us -> 0.03 us  [exchange_form(): (keep[quarter:] + near[quarter:].astype(jnp.float32)).astype(jnp.bfloat16)]
  transfers between devices with their start and end apart: 4 -> 5, of which waited for: 4 -> 5; matrix products, arithmetic and copies ran while one was open for 0% -> 2% of each run, Pallas kernels for 0% -> 1%
where the time goes in v2:
time: 38.4 us; the launch traced here: 37.8 us
  starting transfers between devices  15.6 us (41%)
  waiting for transfers between devices  12.9 us (34%)
  Pallas kernels  4.48 us (12%)
  local copies, waits for them, and re-layouts  3.97 us (10%)
  other arithmetic  0.73 us (2%)
    all_to_all x1, starting transfers between devices, exchange_form(): arrived = lax.all_to_all(outgoing, 'seq', 0, 0)  7.29 us
    all_to_all x1, waiting for transfers between devices, exchange_form(): arrived = lax.all_to_all(outgoing, 'seq', 0, 0)  5.5 us
    ppermute x1, waiting for transfers between devices, exchange_form(): far = lax.ppermute(onward, 'chan', [(c, c ^ 2) for c in range(4)])  4.02 us
    all_to_all x1, starting transfers between devices, exchange_form(): returned = lax.all_to_all(made, 'seq', 0, 0, axis_index_groups=same_part)  3.34 us
    ppermute x1, starting transfers between devices, shifted(): return lax.ppermute(array, axis, pairs)  3.31 us
    unnamed x6, local copies, waits for them, and re-layouts  3.27 us
    pallas_call x1, Pallas kernels, exchange_form(): pl.pallas_call(functools.partial(gate_kernel, copies), out_shape=jax.Shap...  2.13 us
    ppermute x1, starting transfers between devices, exchange_form(): far = lax.ppermute(onward, 'chan', [(c, c ^ 2) for c in range(4)])  1.58 us
  transfers between devices with their start and end apart: 5, of which 5 were waited for; matrix products, arithmetic and copies ran while one was open for 2% of the time, Pallas kernels for 1%

profile of v2, /device:TPU:0, one launch (start us, length us, event | category | flops | bytes accessed | tf_op | source)
XLA Modules:
  0.0 37.8 jit_solution(6315510018376273926)
XLA Ops:
  0.0 2.1 %gate.1 = bf16[8,136,128]{2,1,0:T(8,128)(2,1)} custom-call(bf16[3,128,512]{2,1,0:T(8,128)(2,1)} %bitcast.5, bf16[3,4,3]{2,1,0:T(4,128)(2,1)} %short_hbm.3, bf16[4,96]{1,0:T(4,128)(2,1)} %long_hbm.1), custom_call_target="tpu_custom_call" | custom-call | flops 786432 | bytes 524288 | tf_op jit(solution)/shard_map/gate/pallas_call | solution.py:271
  2.1 7.3 %all-to-all-start = ((bf16[8,136,128]{2,1,0:T(8,128)(2,1)}), bf16[8,136,128]{2,1,0:T(8,128)(2,1)S(1)}, u32[]{:S(2)}, u32[]{:S(2)}) async-start(bf16[8,136,128]{2,1,0:T(8,128)(2,1)} %gate.1), calls=%async_computation | async-start | bytes 557056 | tf_op jit(solution)/shard_map/all_to_all | solution.py:288
  9.4 0.0 copy-start
  9.4 1.6 %copy-done = bf16[512,2048]{1,0:T(8,128)(2,1)S(1)} copy-done((bf16[512,2048]{1,0:T(8,128)(2,1)S(1)}, bf16[512,2048]{1,0:T(8,128)(2,1)}, u32[]{:S(2)}) %copy-start) | copy-done | bytes 2097176
  11.0 0.0 copy-start.1
  11.0 1.0 %copy-done.1 = bf16[128,3,512]{2,0,1:T(8,128)(2,1)S(1)} copy-done((bf16[128,3,512]{2,0,1:T(8,128)(2,1)S(1)}, bf16[128,3,512]{2,0,1:T(8,128)(2,1)}, u32[]{:S(2)}) %copy-start.1) | copy-done | bytes 393240
  12.0 0.0 copy-start.2
  12.0 0.7 %copy-done.2 = bf16[3,4,3]{2,1,0:T(4,128)(2,1)S(1)} copy-done((bf16[3,4,3]{2,1,0:T(4,128)(2,1)S(1)}, bf16[3,4,3]{2,1,0:T(4,128)(2,1)}, u32[]{:S(2)}) %copy-start.2) | copy-done | bytes 96
  12.7 0.5 %ready.1 = (f32[128,512]{1,0:T(8,128)S(1)}, f32[3,4,3]{2,1,0:T(4,128)S(1)}, bf16[512,2048]{1,0:T(8,128)(2,1)S(1)}) custom-call(bf16[3,128,512]{2,1,0:T(8,128)(2,1)S(1)} %bitcast.6, bf16[3,4,3]{2,1,0:T(4,128)(2,1)S(1)} %copy-done.2, bf16[512,2048]{1,0:T(8,128)(2,1)S(1)} %copy-done), custom_call_target="tpu_custom_call" | custom-call | flops 393216 | bytes 2490368 | tf_op jit(solution)/shard_map/ready/pallas_call | solution.py:290
  13.2 5.5 %all-to-all-done.in_ref = bf16[8,136,128]{2,1,0:T(8,128)(2,1)S(1)} async-done(((bf16[8,136,128]{2,1,0:T(8,128)(2,1)}), bf16[8,136,128]{2,1,0:T(8,128)(2,1)S(1)}, u32[]{:S(2)}, u32[]{:S(2)}) %all-to-all-start) | async-done | bytes 278560 | tf_op jit(solution)/shard_map/all_to_all | solution.py:288
  18.7 1.4 %long_filter.1 = bf16[4,128,128]{2,1,0:T(8,128)(2,1)} custom-call(s32[1]{0:T(128)} %bitcast.1.place_ref, bf16[8,136,128]{2,1,0:T(8,128)(2,1)S(1)} %all-to-all-done.in_ref, f32[3,4,3]{2,1,0:T(4,128)S(1)} %get-tuple-element.10.table_ref), custom_call_target="tpu_custom_call" | custom-call | flops 117440512 | bytes 524288 | tf_op jit(solution)/shard_map/long_filter/pallas_call | solution.py:310
  20.1 3.3 %all-to-all-start.1 = ((bf16[4,128,128]{2,1,0:T(8,128)(2,1)}), bf16[4,128,128]{2,1,0:T(8,128)(2,1)S(1)}, u32[]{:S(2)}, u32[]{:S(2)}) async-start(bf16[4,128,128]{2,1,0:T(8,128)(2,1)} %long_filter.1), calls=%async_computation.1 | async-start | bytes 262144 | tf_op jit(solution)/shard_map/all_to_all | solution.py:327
  23.4 0.7 %slice_bitcast_fusion = bf16[2,512]{1,0:T(2,128)(2,1)S(1)} fusion(bf16[128,3,512]{2,0,1:T(8,128)(2,1)} %param.4), kind=kLoop, calls=%fused_computation.2 | loop fusion | bytes 4096 | tf_op jit(solution)/shard_map/squeeze | solution.py:308
  24.1 3.3 %collective-permute-start = (bf16[2,512]{1,0:T(2,128)(2,1)S(1)}, bf16[2,512]{1,0:T(2,128)(2,1)S(1)}, u32[]{:S(2)}, u32[]{:S(2)}) collective-permute-start(bf16[2,512]{1,0:T(2,128)(2,1)S(1)} %slice_bitcast_fusion), channel_id=1, source_target_pairs={{0,4},{4,8},{8,12},{12,16},{16,20},{20,24},{24,28},{1,5},{5,9},{9,... | collective-permute-start | bytes 6152 | tf_op jit(solution)/shard_map/ppermute | solution.py:17
  27.5 1.3 %collective-permute-done.rim_ref = bf16[2,512]{1,0:T(2,128)(2,1)S(1)} collective-permute-done((bf16[2,512]{1,0:T(2,128)(2,1)S(1)}, bf16[2,512]{1,0:T(2,128)(2,1)S(1)}, u32[]{:S(2)}, u32[]{:S(2)}) %collective-permute-start) | collective-permute-done | bytes 2080 | tf_op jit(solution)/shard_map/ppermute | solution.py:17
  28.7 0.6 %all-to-all-done.1.in_ref = bf16[4,128,128]{2,1,0:T(8,128)(2,1)S(1)} async-done(((bf16[4,128,128]{2,1,0:T(8,128)(2,1)}), bf16[4,128,128]{2,1,0:T(8,128)(2,1)S(1)}, u32[]{:S(2)}, u32[]{:S(2)}) %all-to-all-start.1) | async-done | bytes 131104 | tf_op jit(solution)/shard_map/all_to_all | solution.py:327
  29.3 0.5 %project.1 = (bf16[64,2048]{1,0:T(8,128)(2,1)S(1)}, f32[64,2048]{1,0:T(8,128)S(1)}) custom-call(s32[1]{0:T(128)} %bitcast.place_ref, bf16[4,128,128]{2,1,0:T(8,128)(2,1)S(1)} %all-to-all-done.1.in_ref, f32[128,512]{1,0:T(8,128)S(1)} %get-tuple-element.11.query_ref, bf16[2,512]{1,0:T(2,128)(2,1)S(1)} %collective-permute-done.rim_ref, ...), custom_call_target="tpu_custom_call" | custom-call | flops 268435456 | bytes 2097152 | tf_op jit(solution)/shard_map/project/pallas_call | solution.py:329
  29.8 0.1 collective-permute-start.1
  29.9 1.5 %collective-permute-done.1 = bf16[64,2048]{1,0:T(8,128)(2,1)S(1)} collective-permute-done((bf16[64,2048]{1,0:T(8,128)(2,1)S(1)}, bf16[64,2048]{1,0:T(8,128)(2,1)S(1)}, u32[]{:S(2)}, u32[]{:S(2)}) %collective-permute-start.1) | collective-permute-done | bytes 262176 | tf_op jit(solution)/shard_map/ppermute | solution.py:342
  31.4 1.6 %collective-permute-start.2 = (bf16[32,2048]{1,0:T(8,128)(2,1)S(1)}, bf16[32,2048]{1,0:T(8,128)(2,1)S(1)}, u32[]{:S(2)}, u32[]{:S(2)}) collective-permute-start(bf16[32,2048]{1,0:T(8,128)(2,1)S(1)} %add_convert_fusion.1), channel_id=1, source_target_pairs={{0,2},{1,3},{2,0},{3,1},{4,6},{5,7},{6,4},{7,5},{8,10},{9,11},{10,... | collective-permute-start | bytes 393224 | tf_op jit(solution)/shard_map/ppermute | solution.py:345
  33.0 4.0 %collective-permute-done.2 = bf16[32,2048]{1,0:T(8,128)(2,1)S(1)} collective-permute-done((bf16[32,2048]{1,0:T(8,128)(2,1)S(1)}, bf16[32,2048]{1,0:T(8,128)(2,1)S(1)}, u32[]{:S(2)}, u32[]{:S(2)}) %collective-permute-start.2) | collective-permute-done | bytes 131104 | tf_op jit(solution)/shard_map/ppermute | solution.py:345
  37.1 0.7 %add_convert_fusion = bf16[32,2048]{1,0:T(8,128)(2,1)} fusion(bf16[32,2048]{1,0:T(8,128)(2,1)S(1)} %collective-permute-done.2, f32[64,2048]{1,0:T(8,128)S(1)} %get-tuple-element.13, bf16[64,2048]{1,0:T(8,128)(2,1)S(1)} %collective-permute-done.1), kind=kLoop, calls=%fused_computation | loop fusion | flops 327680 | bytes 655360 | tf_op jit(solution)/shard_map/convert_element_type | solution.py:347
  (1 shorter events, 0.0 us)
Async XLA Ops:
  2.1 16.6 %all-to-all-start = ((bf16[8,136,128]{2,1,0:T(8,128)(2,1)}), bf16[8,136,128]{2,1,0:T(8,128)(2,1)S(1)}, u32[]{:S(2)}, u32[]{:S(2)}) async-start(bf16[8,136,128]{2,1,0:T(8,128)(2,1)} %gate.1), calls=%async_computation | async-start | bytes 557056 | tf_op jit(solution)/shard_map/all_to_all | solution.py:288
  9.4 1.6 %copy-start = (bf16[512,2048]{1,0:T(8,128)(2,1)S(1)}, bf16[512,2048]{1,0:T(8,128)(2,1)}, u32[]{:S(2)}) copy-start(bf16[512,2048]{1,0:T(8,128)(2,1)} %weight_hbm.1) | copy-start | bytes 6291460
  11.0 1.0 %copy-start.1 = (bf16[128,3,512]{2,0,1:T(8,128)(2,1)S(1)}, bf16[128,3,512]{2,0,1:T(8,128)(2,1)}, u32[]{:S(2)}) copy-start(bf16[128,3,512]{2,0,1:T(8,128)(2,1)} %param.4) | copy-start | bytes 1179652
  12.0 0.7 %copy-start.2 = (bf16[3,4,3]{2,1,0:T(4,128)(2,1)S(1)}, bf16[3,4,3]{2,1,0:T(4,128)(2,1)}, u32[]{:S(2)}) copy-start(bf16[3,4,3]{2,1,0:T(4,128)(2,1)} %short_hbm.3) | copy-start | bytes 220
  20.1 9.2 %all-to-all-start.1 = ((bf16[4,128,128]{2,1,0:T(8,128)(2,1)}), bf16[4,128,128]{2,1,0:T(8,128)(2,1)S(1)}, u32[]{:S(2)}, u32[]{:S(2)}) async-start(bf16[4,128,128]{2,1,0:T(8,128)(2,1)} %long_filter.1), calls=%async_computation.1 | async-start | bytes 262144 | tf_op jit(solution)/shard_map/all_to_all | solution.py:327
  24.1 4.6 %collective-permute-start = (bf16[2,512]{1,0:T(2,128)(2,1)S(1)}, bf16[2,512]{1,0:T(2,128)(2,1)S(1)}, u32[]{:S(2)}, u32[]{:S(2)}) collective-permute-start(bf16[2,512]{1,0:T(2,128)(2,1)S(1)} %slice_bitcast_fusion), channel_id=1, source_target_pairs={{0,4},{4,8},{8,12},{12,16},{16,20},{20,24},{24,28},{1,5},{5,9},{9,... | collective-permute-start | bytes 6152 | tf_op jit(solution)/shard_map/ppermute | solution.py:17
  29.8 1.6 %collective-permute-start.1 = (bf16[64,2048]{1,0:T(8,128)(2,1)S(1)}, bf16[64,2048]{1,0:T(8,128)(2,1)S(1)}, u32[]{:S(2)}, u32[]{:S(2)}) collective-permute-start(bf16[64,2048]{1,0:T(8,128)(2,1)S(1)} %get-tuple-element.14), channel_id=1, source_target_pairs={{0,1},{1,0},{2,3},{3,2},{4,5},{5,4},{6,7},{7,6},{8,9},{9,8},{10,11... | collective-permute-start | bytes 786440 | tf_op jit(solution)/shard_map/ppermute | solution.py:342
  31.4 5.6 %collective-permute-start.2 = (bf16[32,2048]{1,0:T(8,128)(2,1)S(1)}, bf16[32,2048]{1,0:T(8,128)(2,1)S(1)}, u32[]{:S(2)}, u32[]{:S(2)}) collective-permute-start(bf16[32,2048]{1,0:T(8,128)(2,1)S(1)} %add_convert_fusion.1), channel_id=1, source_target_pairs={{0,2},{1,3},{2,0},{3,1},{4,6},{5,7},{6,4},{7,5},{8,10},{9,11},{10,... | collective-permute-start | bytes 393224 | tf_op jit(solution)/shard_map/ppermute | solution.py:345

commit v3 on v2

v3 whole, which is shorter than its diff:
```python
import functools

import jax
import jax.numpy as jnp
from jax import lax
from jax.experimental import pallas as pl
from jax.experimental.pallas import tpu as pltpu
from jax.sharding import PartitionSpec as P

REACH = 6
EXTRA = 16
RIM = 8


def shifted(array, axis, by):
    peers = lax.axis_size(axis)
    pairs = [(i, i + by) for i in range(peers) if 0 <= i + by < peers]
    return lax.ppermute(array, axis, pairs)


def toeplitz_block(padded, offset, row_count):
    group_count = padded.shape[0]
    window = lax.slice_in_dim(
        padded, offset * row_count + 1, offset * row_count + 2 * row_count, axis=1
    )
    tiled_rows = jnp.tile(window, (1, row_count + 1))[:, : 2 * row_count * row_count]
    tiled_rows = tiled_rows.reshape(group_count, row_count, 2 * row_count)
    return tiled_rows[:, :, :row_count][:, :, ::-1]


def ring_form(projected, short_filter, long_filter, out_weight):
    row_count, _, chan_count = projected.shape
    tap_count = short_filter.shape[-1]
    group_count = short_filter.shape[1]
    group_width = chan_count // group_count
    tail_rows = projected[row_count - tap_count + 1 :]
    arrived_rim = shifted(tail_rows, "seq", 1)
    padded_rows = jnp.concatenate([arrived_rim, projected], axis=0)
    channel_taps = jnp.repeat(short_filter.astype(jnp.float32), group_width, axis=1)
    streams = jnp.zeros((row_count, 3, chan_count), jnp.float32)
    for lag in range(tap_count):
        begin = tap_count - 1 - lag
        window = lax.slice_in_dim(padded_rows, begin, begin + row_count, axis=0)
        streams = streams + channel_taps[None, :, :, lag] * window.astype(jnp.float32)
    query_part = streams[:, 0]
    gated_input = (streams[:, 1] * streams[:, 2]).astype(jnp.bfloat16)
    filters = lax.all_gather(long_filter, "seq", axis=1, tiled=True)
    padded = jnp.pad(filters, ((0, 0), (row_count, row_count)))

    def add_offset(running, offset, source_block):
        matrix = toeplitz_block(padded, offset, row_count)
        shaped_block = source_block.reshape(row_count, group_count, group_width)
        return running + jnp.einsum(
            "gij,jgc->igc", matrix, shaped_block, preferred_element_type=jnp.float32
        )

    running = add_offset(
        jnp.zeros((row_count, group_count, group_width), jnp.float32), 0, gated_input
    )
    moving = gated_input
    for offset in range(1, REACH + 1):
        moving = shifted(moving, "seq", 1)
        running = add_offset(running, offset, moving)
    mixed_out = (query_part * running.reshape(row_count, chan_count)).astype(jnp.bfloat16)
    result = lax.psum_scatter(
        jnp.dot(mixed_out, out_weight, preferred_element_type=jnp.float32),
        "chan",
        scatter_dimension=0,
        tiled=True,
    )
    return result.astype(jnp.bfloat16)


def lagged(stream, lag):
    moved = pltpu.roll(stream, lag, axis=0)
    rows = lax.broadcasted_iota(jnp.int32, stream.shape, 0)
    return jnp.where(rows >= lag, moved, 0.0)


def taps_of(table, group):
    rows = lax.broadcasted_iota(jnp.int32, table.shape, 0)
    row = jnp.sum(jnp.where(rows == group, table, 0.0), axis=0, keepdims=True)
    return [row[:, m : m + 1] for m in range(3)]


def short_sum(stream, tap):
    return tap[0] * stream + tap[1] * lagged(stream, 1) + tap[2] * lagged(stream, 2)


def gate_kernel(copies, place_ref, proj_hbm, short_hbm, long_hbm, *refs):
    group_count, row_count = long_hbm.shape[0], proj_hbm.shape[1]
    out_refs, table_ref = refs[:group_count], refs[group_count]
    proj_ref, short_ref, long_ref, extra_ref, tail_ref, sems = refs[group_count + 1 :]
    width = proj_ref.shape[-1]
    lags = long_ref.shape[1]
    mine = place_ref[0] // copies
    small = [
        pltpu.make_async_copy(short_hbm, short_ref, sems.at[0]),
        pltpu.make_async_copy(long_hbm, long_ref, sems.at[1]),
        pltpu.make_async_copy(proj_hbm.at[0, row_count - 8 :], tail_ref, sems.at[2]),
    ]
    order = list(range(group_count))[::-1]
    large = {}
    for d in order:
        lanes = pl.ds(pl.multiple_of((mine ^ d) * width, width), width)
        large[d] = pltpu.make_async_copy(proj_hbm.at[1:3, :, lanes], proj_ref.at[d], sems.at[3 + d])
    for copy in small + [large[d] for d in order]:
        copy.start()
    extra_ref[...] = jnp.zeros_like(extra_ref)
    for copy in small:
        copy.wait()
    tables = [short_ref[s].astype(jnp.float32) for s in (1, 2)]
    for s in range(3):
        table_ref[s] = short_ref[s].astype(jnp.float32)
    long_rows = long_ref[...].astype(jnp.float32)
    long_row_ids = lax.broadcasted_iota(jnp.int32, long_rows.shape, 0)
    for d in order:
        group = mine ^ d
        taps = [taps_of(table, group) for table in tables]
        picked = jnp.where(long_row_ids == group, long_rows, 0.0)
        extra_ref[d, 0:1, 0:lags] = jnp.sum(picked, axis=0, keepdims=True)
        large[d].wait()
        key, value = (proj_ref[d, s].astype(jnp.float32) for s in range(2))
        gated = short_sum(key, taps[0]) * short_sum(value, taps[1])
        rows = lax.broadcasted_iota(jnp.int32, gated.shape, 0)
        extra_ref[d, 1:3] = value[0:2]
        extra_ref[d, 3:5] = key[row_count - 2 :]
        extra_ref[d, 5:7] = value[row_count - 2 :]
        lanes = pl.ds(pl.multiple_of(group * width, width), width)
        extra_ref[d, 8:10] = tail_ref[:, lanes].astype(jnp.float32)[6:8]
        out_refs[d][0:row_count] = jnp.where(rows < 2, key, gated).astype(jnp.bfloat16)
        out_refs[d][row_count:] = extra_ref[d].astype(jnp.bfloat16)


def ready_kernel(proj_hbm, weight_hbm, table_ref, query_ref, weight_ref, proj_ref, sems):
    copies = [
        pltpu.make_async_copy(proj_hbm.at[0], proj_ref, sems.at[0]),
        pltpu.make_async_copy(weight_hbm, weight_ref, sems.at[1]),
    ]
    for copy in copies:
        copy.start()
    table = table_ref[0]
    group_count = table.shape[0]
    width = query_ref.shape[1] // group_count
    copies[0].wait()
    for g in range(group_count):
        lanes = slice(g * width, (g + 1) * width)
        query_ref[:, lanes] = short_sum(proj_ref[:, lanes].astype(jnp.float32), taps_of(table, g))
    copies[1].wait()


def filter_kernel(copies, lags, place_ref, table_ref, *refs):
    seq_count = (len(refs) - 2) * copies // (copies + 1)
    group_count = seq_count // copies
    in_refs, out_refs = refs[:seq_count], refs[seq_count : seq_count + group_count]
    gated_ref, extra_ref = refs[seq_count + group_count :]
    rows_sent, width = in_refs[0].shape
    row_count = rows_sent - EXTRA
    depth = REACH * row_count
    me = place_ref[0]
    group, part = me // copies, me % copies

    gated_ref[0:depth] = jnp.zeros((depth, width), jnp.bfloat16)
    for d in range(group_count):
        for x in range(copies):
            source = (group ^ d) * copies + (part ^ x)
            block = in_refs[x * group_count + d]
            base = pl.multiple_of(depth + source * row_count, row_count)
            gated_ref[pl.ds(base, row_count), :] = block[0:row_count]
            extra_ref[source] = block[row_count:].astype(jnp.float32)

    extras = [extra_ref[s] for s in range(seq_count)]
    lags_back = jnp.concatenate([e[0:1] for e in extras[::-1]], axis=0).astype(jnp.bfloat16)
    i = lax.broadcasted_iota(jnp.int32, (width, width), 0)
    k = lax.broadcasted_iota(jnp.int32, (width, width), 1)
    flip = jnp.where(i + k == lags - 1, 1.0, 0.0).astype(jnp.bfloat16)
    turned = jnp.dot(lags_back, flip, preferred_element_type=jnp.float32)
    span = depth + 2 * row_count
    first_lane = depth - lags * seq_count + 1
    blank = jnp.zeros((1, span - width), jnp.float32)
    line = jnp.zeros((1, span), jnp.float32)
    for s in range(seq_count):
        piece = jnp.concatenate([turned[s : s + 1], blank], axis=1)
        line = line + pltpu.roll(piece, first_lane + lags * s, axis=1)
    strip = pltpu.roll(
        jnp.broadcast_to(line, (row_count, span)), 0, axis=1, stride=1, stride_axis=0
    )
    strip = strip[:, : depth + row_count].astype(jnp.bfloat16)

    taps = [taps_of(table_ref[s], group) for s in (1, 2)]
    tile_rows = lax.broadcasted_iota(jnp.int32, (16, width), 0)
    before = jnp.zeros((EXTRA, width), jnp.float32)
    for s in range(seq_count):
        here = extras[s]
        base = depth + s * row_count
        tile = gated_ref[base : base + 16].astype(jnp.float32)
        heads = []
        for stream, head in enumerate((tile[0:2], here[1:3])):
            tap = taps[stream]
            first, second = head[0:1], head[1:2]
            older, newer = before[3 + 2 * stream : 4 + 2 * stream], before[4 + 2 * stream : 5 + 2 * stream]
            heads.append(
                (
                    tap[0] * first + tap[1] * newer + tap[2] * older,
                    tap[0] * second + tap[1] * first + tap[2] * newer,
                )
            )
        tile = jnp.where(tile_rows == 0, heads[0][0] * heads[1][0], tile)
        tile = jnp.where(tile_rows == 1, heads[0][1] * heads[1][1], tile)
        gated_ref[base : base + 16] = tile.astype(jnp.bfloat16)
        before = here

    for d in range(group_count):
        block = (group ^ d) * copies + part
        start = pl.multiple_of(block * row_count, row_count)
        source = gated_ref[pl.ds(start, depth + row_count), :]
        made = jnp.dot(strip, source, preferred_element_type=jnp.float32)
        out_refs[d][0:row_count] = made.astype(jnp.bfloat16)
        rim = jnp.where(block > 0, extra_ref[jnp.maximum(block - 1, 0), 8:], 0.0)
        out_refs[d][row_count:] = rim.astype(jnp.bfloat16)


def project_kernel(copies, seq_ref, place_ref, query_ref, table_ref, weight_ref, *refs):
    in_refs, (send_ref, keep_ref, mixed_ref) = refs[:-3], refs[-3:]
    row_count, width = in_refs[0].shape[0] - RIM, in_refs[0].shape[1]
    rows = lax.broadcasted_iota(jnp.int32, (8, width), 0)
    for d, long_ref in enumerate(in_refs):
        group = (seq_ref[0] // copies) ^ d
        lanes = pl.ds(pl.multiple_of(group * width, width), width)
        rim = long_ref[row_count:].astype(jnp.float32)
        older, newer = rim[0:1], rim[1:2]
        _, one, two = taps_of(table_ref[0], group)
        head = query_ref[0:8, lanes]
        head = head + jnp.where(rows == 0, one * newer + two * older, 0.0)
        head = head + jnp.where(rows == 1, two * newer, 0.0)
        query = jnp.concatenate([head, query_ref[8:, lanes]], axis=0)
        mixed_ref[:, lanes] = (query * long_ref[0:row_count].astype(jnp.float32)).astype(jnp.bfloat16)
    quarter = row_count // 4
    me = place_ref[0]

    def take(member):
        return mixed_ref[pl.ds(pl.multiple_of(member * quarter, quarter), quarter), :]

    ordered = jnp.concatenate([take(me ^ 1), take(me ^ 3), take(me), take(me ^ 2)], axis=0)
    step = 512
    for c in range(0, weight_ref.shape[1], step):
        made = jnp.dot(
            ordered, weight_ref[:, c : c + step], preferred_element_type=jnp.float32
        )
        send_ref[:, c : c + step] = made[: 2 * quarter].astype(jnp.bfloat16)
        keep_ref[:, c : c + step] = made[2 * quarter :]


def room(mib):
    return pltpu.CompilerParams(vmem_limit_bytes=mib << 20)


def cost(flops, moved):
    return pl.CostEstimate(flops=flops, bytes_accessed=moved, transcendentals=0)


def whole(space=pltpu.VMEM):
    return pl.BlockSpec(memory_space=space)


def in_hbm(array):
    return pltpu.with_memory_space_constraint(array, pltpu.HBM)


def swapped(array, axis, flip):
    return lax.ppermute(array, axis, [(i, i ^ flip) for i in range(lax.axis_size(axis))])


def exchange_form(projected, short_filter, long_filter, out_weight):
    row_count, _, chan_count = projected.shape
    group_count = short_filter.shape[1]
    width = chan_count // group_count
    out_count = out_weight.shape[1]
    seq_count = lax.axis_size("seq")
    copies = seq_count // group_count
    lags = long_filter.shape[1]
    rows_sent = row_count + EXTRA
    streams = in_hbm(jnp.transpose(projected, (1, 0, 2)))
    seq_place = lax.axis_index("seq").astype(jnp.int32).reshape(1)
    chan_place = lax.axis_index("chan").astype(jnp.int32).reshape(1)
    block_bytes = row_count * chan_count * 2

    *outgoing, table = pl.pallas_call(
        functools.partial(gate_kernel, copies),
        out_shape=[jax.ShapeDtypeStruct((rows_sent, width), jnp.bfloat16)] * group_count
        + [jax.ShapeDtypeStruct(short_filter.shape, jnp.float32)],
        in_specs=[whole(pltpu.SMEM)] + [whole(pltpu.HBM)] * 3,
        out_specs=[whole()] * (group_count + 1),
        scratch_shapes=[
            pltpu.VMEM((group_count, 2, row_count, width), projected.dtype),
            pltpu.VMEM(short_filter.shape, short_filter.dtype),
            pltpu.VMEM(long_filter.shape, long_filter.dtype),
            pltpu.VMEM((group_count, EXTRA, width), jnp.float32),
            pltpu.VMEM((8, chan_count), projected.dtype),
            pltpu.SemaphoreType.DMA((3 + group_count,)),
        ],
        compiler_params=room(4),
        cost_estimate=cost(12 * row_count * chan_count, 4 * block_bytes),
        name="gate",
    )(seq_place, streams, in_hbm(short_filter), in_hbm(long_filter))
    mine = list(outgoing)
    for d in range(group_count - 1, 0, -1):
        mine[d] = swapped(mine[d], "seq", d * copies)
    other = [swapped(block, "seq", 1) for block in mine]

    query, weight = pl.pallas_call(
        ready_kernel,
        out_shape=(
            jax.ShapeDtypeStruct((row_count, chan_count), jnp.float32),
            jax.ShapeDtypeStruct(out_weight.shape, out_weight.dtype),
        ),
        in_specs=[whole(pltpu.HBM)] * 2 + [whole()],
        out_specs=(whole(), whole()),
        scratch_shapes=[
            pltpu.VMEM((row_count, chan_count), projected.dtype),
            pltpu.SemaphoreType.DMA((2,)),
        ],
        compiler_params=room(4),
        cost_estimate=cost(6 * row_count * chan_count, 2 * chan_count * out_count + 3 * block_bytes),
        name="ready",
    )(streams, in_hbm(out_weight), table)

    made = pl.pallas_call(
        functools.partial(filter_kernel, copies, lags),
        out_shape=[jax.ShapeDtypeStruct((row_count + RIM, width), jnp.bfloat16)] * group_count,
        in_specs=[whole(pltpu.SMEM)] + [whole()] * (1 + seq_count),
        out_specs=[whole()] * group_count,
        scratch_shapes=[
            pltpu.VMEM(((REACH + seq_count) * row_count, width), jnp.bfloat16),
            pltpu.VMEM((seq_count, EXTRA, width), jnp.float32),
        ],
        compiler_params=room(4),
        cost_estimate=cost(
            2 * group_count * (REACH + 1) * row_count * row_count * width, 4 * block_bytes
        ),
        name="long_filter",
    )(seq_place, table, *mine, *other)
    returned = list(made)
    for d in range(group_count - 1, 0, -1):
        returned[d] = swapped(returned[d], "seq", d * copies)

    half = row_count // 2
    send, keep = pl.pallas_call(
        functools.partial(project_kernel, copies),
        out_shape=(
            jax.ShapeDtypeStruct((half, out_count), jnp.bfloat16),
            jax.ShapeDtypeStruct((half, out_count), jnp.float32),
        ),
        in_specs=[whole(pltpu.SMEM)] * 2 + [whole()] * (3 + group_count),
        out_specs=(whole(), whole()),
        scratch_shapes=[pltpu.VMEM((row_count, chan_count), jnp.bfloat16)],
        compiler_params=room(4),
        cost_estimate=cost(2 * row_count * chan_count * out_count, 2 * chan_count * out_count),
        name="project",
    )(seq_place, chan_place, query, table, weight, *returned)
    near = swapped(send, "chan", 1)
    quarter = half // 2
    onward = (keep[quarter:] + near[quarter:].astype(jnp.float32)).astype(jnp.bfloat16)
    far = swapped(onward, "chan", 2)
    kept = keep[:quarter] + near[:quarter].astype(jnp.float32)
    return (kept + far.astype(jnp.float32)).astype(jnp.bfloat16)


def on_device(projected, short_filter, long_filter, out_weight):
    row_count, _, chan_count = projected.shape
    group_count = short_filter.shape[1]
    width = chan_count // group_count
    seq_count = lax.axis_size("seq")
    exchanged = 3 * group_count * (row_count + EXTRA) * width
    ringed = REACH * row_count * chan_count
    fits = (
        seq_count == 2 * group_count
        and group_count in (2, 4, 8)
        and seq_count * long_filter.shape[1] <= REACH * row_count
        and long_filter.shape[1] <= width
        and width == 128
        and row_count % 64 == 0
        and short_filter.shape[-1] == 3
        and lax.axis_size("chan") == 4
    )
    form = exchange_form if fits and exchanged < ringed else ring_form
    return form(projected, short_filter, long_filter, out_weight)


def solution(mesh):
    return jax.shard_map(
        on_device,
        mesh=mesh,
        in_specs=(P("seq", None, "chan"), P(None, "chan", None), P("chan", "seq"), P("chan", None)),
        out_specs=P(("seq", "chan"), None),
        check_vma=False,
    )
```

time: 38.4 us -> 34.1 us (0.89); the launches traced: 37.8 us -> 33.9 us
  local copies, waits for them, and re-layouts: 3.97 us -> 0 us
  starting transfers between devices: 15.6 us -> 16.8 us
  waiting for transfers between devices: 12.9 us -> 12 us
    ppermute x3 -> x12, starting transfers between devices: 4.97 us -> 16.8 us  [swapped(): lax.ppermute(array, axis, [(i, i ^ flip) for i in range(lax.axis_size(axi...]
    all_to_all x2 -> x0, starting transfers between devices: 10.6 us -> none  [the longest x1 7.29 us: exchange_form(): arrived = lax.all_to_all(outgoing, 'seq', 0, 0)]
    all_to_all x2 -> x0, waiting for transfers between devices: 6.06 us -> none  [the longest x1 5.5 us: exchange_form(): arrived = lax.all_to_all(outgoing, 'seq', 0, 0)]
    ppermute x3 -> x12, waiting for transfers between devices: 6.83 us -> 12 us  [swapped(): lax.ppermute(array, axis, [(i, i ^ flip) for i in range(lax.axis_size(axi...]
    unnamed x6 -> x0, local copies, waits for them, and re-layouts: 3.27 us -> none
    pallas_call x1, Pallas kernels: 0.48 us -> 1.69 us  [exchange_form(): pl.pallas_call(ready_kernel, out_shape=(jax.ShapeDtypeStruct((row_count,...]
    pallas_call x2, Pallas kernels: 2.63 us -> 1.86 us  [the longest x1 1.33 us: exchange_form(): pl.pallas_call(functools.partial(gate_kernel, copies), out_shape=[jax.Sha...]
    squeeze x1 -> x0, local copies, waits for them, and re-layouts: 0.71 us -> none  [exchange_form(): rim = shifted(projected[row_count - 2:, 0], 'seq', 1)]
  transfers between devices with their start and end apart: 5 -> 12, of which waited for: 5 -> 6; matrix products, arithmetic and copies ran while one was open for 2% -> 0% of each run, Pallas kernels for 1% -> 5%
where the time goes in v3:
time: 34.1 us; the launch traced here: 33.9 us
  starting transfers between devices  16.8 us (49%)
  waiting for transfers between devices  12 us (35%)
  Pallas kernels  4.27 us (13%)
  other arithmetic  0.72 us (2%)
    ppermute x12, starting transfers between devices, swapped(): lax.ppermute(array, axis, [(i, i ^ flip) for i in range(lax.axis_size(axi...  16.8 us
    ppermute x12, waiting for transfers between devices, swapped(): lax.ppermute(array, axis, [(i, i ^ flip) for i in range(lax.axis_size(axi...  12 us
    pallas_call x1, Pallas kernels, exchange_form(): pl.pallas_call(ready_kernel, out_shape=(jax.ShapeDtypeStruct((row_count,...  1.69 us
    pallas_call x1, Pallas kernels, exchange_form(): pl.pallas_call(functools.partial(gate_kernel, copies), out_shape=[jax.Sha...  1.33 us
    pallas_call x1, Pallas kernels, exchange_form(): pl.pallas_call(functools.partial(filter_kernel, copies, lags), out_shape=...  0.73 us
    convert_element_type x1, other arithmetic, exchange_form(): return (kept + far.astype(jnp.float32)).astype(jnp.bfloat16)  0.7 us
  transfers between devices with their start and end apart: 12, of which 6 were waited for; matrix products, arithmetic and copies ran while one was open for 0% of the time, Pallas kernels for 5%

profile of v3, /device:TPU:0, one launch (start us, length us, event | category | flops | bytes accessed | tf_op | source)
XLA Modules:
  0.0 33.9 jit_solution(10551117056871566322)
XLA Ops:
  0.0 1.3 %gate.1 = (bf16[144,128]{1,0:T(8,128)(2,1)S(1)}, bf16[144,128]{1,0:T(8,128)(2,1)S(1)}, bf16[144,128]{1,0:T(8,128)(2,1)S(1)}, bf16[144,128]{1,0:T(8,128)(2,1)S(1)}, f32[3,4,3]{2,1,0:T(4,128)S(1)}) custom-call(s32[1]{0:T(128)} %bitcast.place_ref.seq_ref, bf16[3,128,512]{2,1,0:T(8,128)(2,1)} %bitcast.3, bf16[3,4,3]{2,1,0:T(4,128)(2,1)} %short_hbm.1, ...), custom_call_target="tpu_custom_call" | custom-call | flops 786432 | bytes 524288 | tf_op jit(solution)/shard_map/gate/pallas_call | solution.py:288
  1.3 3.1 %collective-permute-start = (bf16[144,128]{1,0:T(8,128)(2,1)S(1)}, bf16[144,128]{1,0:T(8,128)(2,1)S(1)}, u32[]{:S(2)}, u32[]{:S(2)}) collective-permute-start(bf16[144,128]{1,0:T(8,128)(2,1)S(1)} %get-tuple-element.22), channel_id=1, source_target_pairs={{0,8},{4,12},{8,0},{12,4},{16,24},{20,28},{24,16},{28,20},{1,9},{5... | collective-permute-start | bytes 110600 | tf_op jit(solution)/shard_map/ppermute | solution.py:271
  4.5 2.6 %collective-permute-start.1 = (bf16[144,128]{1,0:T(8,128)(2,1)S(1)}, bf16[144,128]{1,0:T(8,128)(2,1)S(1)}, u32[]{:S(2)}, u32[]{:S(2)}) collective-permute-start(bf16[144,128]{1,0:T(8,128)(2,1)S(1)} %get-tuple-element.23), channel_id=1, source_target_pairs={{0,16},{4,20},{8,24},{12,28},{16,0},{20,4},{24,8},{28,12},{1,17},{... | collective-permute-start | bytes 110600 | tf_op jit(solution)/shard_map/ppermute | solution.py:271
  7.0 0.0 collective-permute-start.2
  7.1 1.7 %collective-permute-start.3 = (bf16[144,128]{1,0:T(8,128)(2,1)S(1)}, bf16[144,128]{1,0:T(8,128)(2,1)S(1)}, u32[]{:S(2)}, u32[]{:S(2)}) collective-permute-start(bf16[144,128]{1,0:T(8,128)(2,1)S(1)} %get-tuple-element.21.refs_0_), channel_id=1, source_target_pairs={{0,4},{4,0},{8,12},{12,8},{16,20},{20,16},{24,28},{28,24},{1,5},{5... | collective-permute-start | bytes 110600 | tf_op jit(solution)/shard_map/ppermute | solution.py:271
  8.8 0.0 collective-permute-done.refs_1_
  8.8 0.3 collective-permute-start.4
  9.1 0.9 %collective-permute-done.1.refs_2_ = bf16[144,128]{1,0:T(8,128)(2,1)S(1)} collective-permute-done((bf16[144,128]{1,0:T(8,128)(2,1)S(1)}, bf16[144,128]{1,0:T(8,128)(2,1)S(1)}, u32[]{:S(2)}, u32[]{:S(2)}) %collective-permute-start.1) | collective-permute-done | bytes 36896 | tf_op jit(solution)/shard_map/ppermute | solution.py:271
  10.0 1.5 %collective-permute-start.5 = (bf16[144,128]{1,0:T(8,128)(2,1)S(1)}, bf16[144,128]{1,0:T(8,128)(2,1)S(1)}, u32[]{:S(2)}, u32[]{:S(2)}) collective-permute-start(bf16[144,128]{1,0:T(8,128)(2,1)S(1)} %collective-permute-done.1.refs_2_), channel_id=1, source_target_pairs={{0,4},{4,0},{8,12},{12,8},{16,20},{20,16},{24,28},{28,24},{1,5},{5... | collective-permute-start | bytes 110600 | tf_op jit(solution)/shard_map/ppermute | solution.py:271
  11.5 1.3 %collective-permute-done.2.refs_3_ = bf16[144,128]{1,0:T(8,128)(2,1)S(1)} collective-permute-done((bf16[144,128]{1,0:T(8,128)(2,1)S(1)}, bf16[144,128]{1,0:T(8,128)(2,1)S(1)}, u32[]{:S(2)}, u32[]{:S(2)}) %collective-permute-start.2) | collective-permute-done | bytes 36896 | tf_op jit(solution)/shard_map/ppermute | solution.py:271
  12.8 1.5 %collective-permute-start.6 = (bf16[144,128]{1,0:T(8,128)(2,1)S(1)}, bf16[144,128]{1,0:T(8,128)(2,1)S(1)}, u32[]{:S(2)}, u32[]{:S(2)}) collective-permute-start(bf16[144,128]{1,0:T(8,128)(2,1)S(1)} %collective-permute-done.2.refs_3_), channel_id=1, source_target_pairs={{0,4},{4,0},{8,12},{12,8},{16,20},{20,16},{24,28},{28,24},{1,5},{5... | collective-permute-start | bytes 110600 | tf_op jit(solution)/shard_map/ppermute | solution.py:271
  14.3 2.5 %collective-permute-done.6.refs_7_ = bf16[144,128]{1,0:T(8,128)(2,1)S(1)} collective-permute-done((bf16[144,128]{1,0:T(8,128)(2,1)S(1)}, bf16[144,128]{1,0:T(8,128)(2,1)S(1)}, u32[]{:S(2)}, u32[]{:S(2)}) %collective-permute-start.6) | collective-permute-done | bytes 36896 | tf_op jit(solution)/shard_map/ppermute | solution.py:271
  16.8 0.7 %long_filter.1 = (bf16[136,128]{1,0:T(8,128)(2,1)S(1)}, bf16[136,128]{1,0:T(8,128)(2,1)S(1)}, bf16[136,128]{1,0:T(8,128)(2,1)S(1)}, bf16[136,128]{1,0:T(8,128)(2,1)S(1)}) custom-call(s32[1]{0:T(128)} %bitcast.place_ref.seq_ref, f32[3,4,3]{2,1,0:T(4,128)S(1)} %get-tuple-element.18.table_ref, bf16[144,128]{1,0:T(8,128)(2,1)S(1)} %get-tuple-element.21.refs_0_, ...), custom_call_target="tpu_custom_call" | custom-call | flops 117440512 | bytes 524288 | tf_op jit(solution)/shard_map/long_filter/pallas_call | solution.py:328
  17.5 0.1 collective-permute-start.7
  17.6 2.1 %collective-permute-start.8 = (bf16[136,128]{1,0:T(8,128)(2,1)S(1)}, bf16[136,128]{1,0:T(8,128)(2,1)S(1)}, u32[]{:S(2)}, u32[]{:S(2)}) collective-permute-start(bf16[136,128]{1,0:T(8,128)(2,1)S(1)} %get-tuple-element.27), channel_id=1, source_target_pairs={{0,16},{4,20},{8,24},{12,28},{16,0},{20,4},{24,8},{28,12},{1,17},{... | collective-permute-start | bytes 104456 | tf_op jit(solution)/shard_map/ppermute | solution.py:271
  19.7 2.2 %collective-permute-start.9 = (bf16[136,128]{1,0:T(8,128)(2,1)S(1)}, bf16[136,128]{1,0:T(8,128)(2,1)S(1)}, u32[]{:S(2)}, u32[]{:S(2)}) collective-permute-start(bf16[136,128]{1,0:T(8,128)(2,1)S(1)} %get-tuple-element.28), channel_id=1, source_target_pairs={{0,24},{4,28},{8,16},{12,20},{16,8},{20,12},{24,0},{28,4},{1,25},{... | collective-permute-start | bytes 104456 | tf_op jit(solution)/shard_map/ppermute | solution.py:271
  22.0 1.7 %ready.1 = (f32[128,512]{1,0:T(8,128)S(1)}, bf16[512,2048]{1,0:T(8,128)(2,1)S(1)}) custom-call(bf16[3,128,512]{2,1,0:T(8,128)(2,1)} %bitcast.4, bf16[512,2048]{1,0:T(8,128)(2,1)} %weight_hbm.1, f32[3,4,3]{2,1,0:T(4,128)S(1)} %get-tuple-element.18.table_ref), custom_call_target="tpu_custom_call" | custom-call | flops 393216 | bytes 2490368 | tf_op jit(solution)/shard_map/ready/pallas_call | solution.py:311
  23.7 1.8 %collective-permute-done.9.refs_3_ = bf16[136,128]{1,0:T(8,128)(2,1)S(1)} collective-permute-done((bf16[136,128]{1,0:T(8,128)(2,1)S(1)}, bf16[136,128]{1,0:T(8,128)(2,1)S(1)}, u32[]{:S(2)}, u32[]{:S(2)}) %collective-permute-start.9) | collective-permute-done | bytes 34848 | tf_op jit(solution)/shard_map/ppermute | solution.py:271
  25.5 0.5 %project.1 = (bf16[64,2048]{1,0:T(8,128)(2,1)S(1)}, f32[64,2048]{1,0:T(8,128)S(1)}) custom-call(s32[1]{0:T(128)} %bitcast.place_ref.seq_ref, s32[1]{0:T(128)} %bitcast.1.place_ref, f32[128,512]{1,0:T(8,128)S(1)} %get-tuple-element.19.query_ref, f32[3,4,3]{2,1,0:T(4,128)S(1)} %get-tuple-element.18.table_ref, ...), custom_call_target="tpu_custom_call" | custom-call | flops 268435456 | bytes 2097152 | tf_op jit(solution)/shard_map/project/pallas_call | solution.py:348
  26.0 0.1 collective-permute-start.10
  26.1 1.5 %collective-permute-done.10 = bf16[64,2048]{1,0:T(8,128)(2,1)S(1)} collective-permute-done((bf16[64,2048]{1,0:T(8,128)(2,1)S(1)}, bf16[64,2048]{1,0:T(8,128)(2,1)S(1)}, u32[]{:S(2)}, u32[]{:S(2)}) %collective-permute-start.10) | collective-permute-done | bytes 262176 | tf_op jit(solution)/shard_map/ppermute | solution.py:271
  27.6 1.6 %collective-permute-start.11 = (bf16[32,2048]{1,0:T(8,128)(2,1)S(1)}, bf16[32,2048]{1,0:T(8,128)(2,1)S(1)}, u32[]{:S(2)}, u32[]{:S(2)}) collective-permute-start(bf16[32,2048]{1,0:T(8,128)(2,1)S(1)} %add_convert_fusion.1), channel_id=1, source_target_pairs={{0,2},{1,3},{2,0},{3,1},{4,6},{5,7},{6,4},{7,5},{8,10},{9,11},{10,... | collective-permute-start | bytes 393224 | tf_op jit(solution)/shard_map/ppermute | solution.py:271
  29.2 4.0 %collective-permute-done.11 = bf16[32,2048]{1,0:T(8,128)(2,1)S(1)} collective-permute-done((bf16[32,2048]{1,0:T(8,128)(2,1)S(1)}, bf16[32,2048]{1,0:T(8,128)(2,1)S(1)}, u32[]{:S(2)}, u32[]{:S(2)}) %collective-permute-start.11) | collective-permute-done | bytes 131104 | tf_op jit(solution)/shard_map/ppermute | solution.py:271
  33.2 0.7 %add_convert_fusion = bf16[32,2048]{1,0:T(8,128)(2,1)} fusion(bf16[32,2048]{1,0:T(8,128)(2,1)S(1)} %collective-permute-done.11, f32[64,2048]{1,0:T(8,128)S(1)} %get-tuple-element.29, bf16[64,2048]{1,0:T(8,128)(2,1)S(1)} %collective-permute-done.10), kind=kLoop, calls=%fused_computation | loop fusion | flops 327680 | bytes 655360 | tf_op jit(solution)/shard_map/convert_element_type | solution.py:366
  (6 shorter events, 0.0 us)
Async XLA Ops:
  1.3 7.4 %collective-permute-start = (bf16[144,128]{1,0:T(8,128)(2,1)S(1)}, bf16[144,128]{1,0:T(8,128)(2,1)S(1)}, u32[]{:S(2)}, u32[]{:S(2)}) collective-permute-start(bf16[144,128]{1,0:T(8,128)(2,1)S(1)} %get-tuple-element.22), channel_id=1, source_target_pairs={{0,8},{4,12},{8,0},{12,4},{16,24},{20,28},{24,16},{28,20},{1,9},{5... | collective-permute-start | bytes 110600 | tf_op jit(solution)/shard_map/ppermute | solution.py:271
  4.5 5.5 %collective-permute-start.1 = (bf16[144,128]{1,0:T(8,128)(2,1)S(1)}, bf16[144,128]{1,0:T(8,128)(2,1)S(1)}, u32[]{:S(2)}, u32[]{:S(2)}) collective-permute-start(bf16[144,128]{1,0:T(8,128)(2,1)S(1)} %get-tuple-element.23), channel_id=1, source_target_pairs={{0,16},{4,20},{8,24},{12,28},{16,0},{20,4},{24,8},{28,12},{1,17},{... | collective-permute-start | bytes 110600 | tf_op jit(solution)/shard_map/ppermute | solution.py:271
  7.0 5.8 %collective-permute-start.2 = (bf16[144,128]{1,0:T(8,128)(2,1)S(1)}, bf16[144,128]{1,0:T(8,128)(2,1)S(1)}, u32[]{:S(2)}, u32[]{:S(2)}) collective-permute-start(bf16[144,128]{1,0:T(8,128)(2,1)S(1)} %get-tuple-element.24), channel_id=1, source_target_pairs={{0,24},{4,28},{8,16},{12,20},{16,8},{20,12},{24,0},{28,4},{1,25},{... | collective-permute-start | bytes 110600 | tf_op jit(solution)/shard_map/ppermute | solution.py:271
  7.1 7.2 %collective-permute-start.3 = (bf16[144,128]{1,0:T(8,128)(2,1)S(1)}, bf16[144,128]{1,0:T(8,128)(2,1)S(1)}, u32[]{:S(2)}, u32[]{:S(2)}) collective-permute-start(bf16[144,128]{1,0:T(8,128)(2,1)S(1)} %get-tuple-element.21.refs_0_), channel_id=1, source_target_pairs={{0,4},{4,0},{8,12},{12,8},{16,20},{20,16},{24,28},{28,24},{1,5},{5... | collective-permute-start | bytes 110600 | tf_op jit(solution)/shard_map/ppermute | solution.py:271
  8.8 5.5 %collective-permute-start.4 = (bf16[144,128]{1,0:T(8,128)(2,1)S(1)}, bf16[144,128]{1,0:T(8,128)(2,1)S(1)}, u32[]{:S(2)}, u32[]{:S(2)}) collective-permute-start(bf16[144,128]{1,0:T(8,128)(2,1)S(1)} %collective-permute-done.refs_1_), channel_id=1, source_target_pairs={{0,4},{4,0},{8,12},{12,8},{16,20},{20,16},{24,28},{28,24},{1,5},{5... | collective-permute-start | bytes 110600 | tf_op jit(solution)/shard_map/ppermute | solution.py:271
  10.0 4.3 %collective-permute-start.5 = (bf16[144,128]{1,0:T(8,128)(2,1)S(1)}, bf16[144,128]{1,0:T(8,128)(2,1)S(1)}, u32[]{:S(2)}, u32[]{:S(2)}) collective-permute-start(bf16[144,128]{1,0:T(8,128)(2,1)S(1)} %collective-permute-done.1.refs_2_), channel_id=1, source_target_pairs={{0,4},{4,0},{8,12},{12,8},{16,20},{20,16},{24,28},{28,24},{1,5},{5... | collective-permute-start | bytes 110600 | tf_op jit(solution)/shard_map/ppermute | solution.py:271
  12.8 4.0 %collective-permute-start.6 = (bf16[144,128]{1,0:T(8,128)(2,1)S(1)}, bf16[144,128]{1,0:T(8,128)(2,1)S(1)}, u32[]{:S(2)}, u32[]{:S(2)}) collective-permute-start(bf16[144,128]{1,0:T(8,128)(2,1)S(1)} %collective-permute-done.2.refs_3_), channel_id=1, source_target_pairs={{0,4},{4,0},{8,12},{12,8},{16,20},{20,16},{24,28},{28,24},{1,5},{5... | collective-permute-start | bytes 110600 | tf_op jit(solution)/shard_map/ppermute | solution.py:271
  17.5 6.2 %collective-permute-start.7 = (bf16[136,128]{1,0:T(8,128)(2,1)S(1)}, bf16[136,128]{1,0:T(8,128)(2,1)S(1)}, u32[]{:S(2)}, u32[]{:S(2)}) collective-permute-start(bf16[136,128]{1,0:T(8,128)(2,1)S(1)} %get-tuple-element.26), channel_id=1, source_target_pairs={{0,8},{4,12},{8,0},{12,4},{16,24},{20,28},{24,16},{28,20},{1,9},{5... | collective-permute-start | bytes 104456 | tf_op jit(solution)/shard_map/ppermute | solution.py:271
  17.6 6.1 %collective-permute-start.8 = (bf16[136,128]{1,0:T(8,128)(2,1)S(1)}, bf16[136,128]{1,0:T(8,128)(2,1)S(1)}, u32[]{:S(2)}, u32[]{:S(2)}) collective-permute-start(bf16[136,128]{1,0:T(8,128)(2,1)S(1)} %get-tuple-element.27), channel_id=1, source_target_pairs={{0,16},{4,20},{8,24},{12,28},{16,0},{20,4},{24,8},{28,12},{1,17},{... | collective-permute-start | bytes 104456 | tf_op jit(solution)/shard_map/ppermute | solution.py:271
  19.7 5.7 %collective-permute-start.9 = (bf16[136,128]{1,0:T(8,128)(2,1)S(1)}, bf16[136,128]{1,0:T(8,128)(2,1)S(1)}, u32[]{:S(2)}, u32[]{:S(2)}) collective-permute-start(bf16[136,128]{1,0:T(8,128)(2,1)S(1)} %get-tuple-element.28), channel_id=1, source_target_pairs={{0,24},{4,28},{8,16},{12,20},{16,8},{20,12},{24,0},{28,4},{1,25},{... | collective-permute-start | bytes 104456 | tf_op jit(solution)/shard_map/ppermute | solution.py:271
  26.0 1.6 %collective-permute-start.10 = (bf16[64,2048]{1,0:T(8,128)(2,1)S(1)}, bf16[64,2048]{1,0:T(8,128)(2,1)S(1)}, u32[]{:S(2)}, u32[]{:S(2)}) collective-permute-start(bf16[64,2048]{1,0:T(8,128)(2,1)S(1)} %get-tuple-element.30), channel_id=1, source_target_pairs={{0,1},{1,0},{2,3},{3,2},{4,5},{5,4},{6,7},{7,6},{8,9},{9,8},{10,11... | collective-permute-start | bytes 786440 | tf_op jit(solution)/shard_map/ppermute | solution.py:271
  27.6 5.6 %collective-permute-start.11 = (bf16[32,2048]{1,0:T(8,128)(2,1)S(1)}, bf16[32,2048]{1,0:T(8,128)(2,1)S(1)}, u32[]{:S(2)}, u32[]{:S(2)}) collective-permute-start(bf16[32,2048]{1,0:T(8,128)(2,1)S(1)} %add_convert_fusion.1), channel_id=1, source_target_pairs={{0,2},{1,3},{2,0},{3,1},{4,6},{5,7},{6,4},{7,5},{8,10},{9,11},{10,... | collective-permute-start | bytes 393224 | tf_op jit(solution)/shard_map/ppermute | solution.py:271

commit v4 on v3

--- a/solution.py
+++ b/solution.py
@@ -87,13 +87,13 @@
     return tap[0] * stream + tap[1] * lagged(stream, 1) + tap[2] * lagged(stream, 2)
 
 
-def gate_kernel(copies, place_ref, proj_hbm, short_hbm, long_hbm, *refs):
+def gate_kernel(place_ref, proj_hbm, short_hbm, long_hbm, *refs):
     group_count, row_count = long_hbm.shape[0], proj_hbm.shape[1]
     out_refs, table_ref = refs[:group_count], refs[group_count]
     proj_ref, short_ref, long_ref, extra_ref, tail_ref, sems = refs[group_count + 1 :]
     width = proj_ref.shape[-1]
     lags = long_ref.shape[1]
-    mine = place_ref[0] // copies
+    mine = place_ref[0] % group_count
     small = [
         pltpu.make_async_copy(short_hbm, short_ref, sems.at[0]),
         pltpu.make_async_copy(long_hbm, long_ref, sems.at[1]),
@@ -158,12 +158,12 @@
     row_count = rows_sent - EXTRA
     depth = REACH * row_count
     me = place_ref[0]
-    group, part = me // copies, me % copies
+    group, part = me % group_count, me // group_count
 
     gated_ref[0:depth] = jnp.zeros((depth, width), jnp.bfloat16)
     for d in range(group_count):
         for x in range(copies):
-            source = (group ^ d) * copies + (part ^ x)
+            source = (part ^ x) * group_count + (group ^ d)
             block = in_refs[x * group_count + d]
             base = pl.multiple_of(depth + source * row_count, row_count)
             gated_ref[pl.ds(base, row_count), :] = block[0:row_count]
@@ -211,7 +211,7 @@
         before = here
 
     for d in range(group_count):
-        block = (group ^ d) * copies + part
+        block = part * group_count + (group ^ d)
         start = pl.multiple_of(block * row_count, row_count)
         source = gated_ref[pl.ds(start, depth + row_count), :]
         made = jnp.dot(strip, source, preferred_element_type=jnp.float32)
@@ -220,12 +220,12 @@
         out_refs[d][row_count:] = rim.astype(jnp.bfloat16)
 
 
-def project_kernel(copies, seq_ref, place_ref, query_ref, table_ref, weight_ref, *refs):
+def project_kernel(seq_ref, place_ref, query_ref, table_ref, weight_ref, *refs):
     in_refs, (send_ref, keep_ref, mixed_ref) = refs[:-3], refs[-3:]
     row_count, width = in_refs[0].shape[0] - RIM, in_refs[0].shape[1]
     rows = lax.broadcasted_iota(jnp.int32, (8, width), 0)
     for d, long_ref in enumerate(in_refs):
-        group = (seq_ref[0] // copies) ^ d
+        group = (seq_ref[0] % len(in_refs)) ^ d
         lanes = pl.ds(pl.multiple_of(group * width, width), width)
         rim = long_ref[row_count:].astype(jnp.float32)
         older, newer = rim[0:1], rim[1:2]
@@ -286,7 +286,7 @@
     block_bytes = row_count * chan_count * 2
 
     *outgoing, table = pl.pallas_call(
-        functools.partial(gate_kernel, copies),
+        gate_kernel,
         out_shape=[jax.ShapeDtypeStruct((rows_sent, width), jnp.bfloat16)] * group_count
         + [jax.ShapeDtypeStruct(short_filter.shape, jnp.float32)],
         in_specs=[whole(pltpu.SMEM)] + [whole(pltpu.HBM)] * 3,
@@ -303,10 +303,13 @@
         cost_estimate=cost(12 * row_count * chan_count, 4 * block_bytes),
         name="gate",
     )(seq_place, streams, in_hbm(short_filter), in_hbm(long_filter))
-    mine = list(outgoing)
-    for d in range(group_count - 1, 0, -1):
-        mine[d] = swapped(mine[d], "seq", d * copies)
-    other = [swapped(block, "seq", 1) for block in mine]
+    mine, other = list(outgoing), [None] * group_count
+    for d in (1, 3, 2):
+        mine[d] = swapped(mine[d], "seq", d)
+    for pair in ((0, 1), (3, 2)):
+        both = swapped(jnp.concatenate([mine[d] for d in pair]), "seq", group_count)
+        for i, d in enumerate(pair):
+            other[d] = both[i * rows_sent : (i + 1) * rows_sent]
 
     query, weight = pl.pallas_call(
         ready_kernel,
@@ -341,12 +344,12 @@
         name="long_filter",
     )(seq_place, table, *mine, *other)
     returned = list(made)
-    for d in range(group_count - 1, 0, -1):
-        returned[d] = swapped(returned[d], "seq", d * copies)
+    for d in (3, 2, 1):
+        returned[d] = swapped(returned[d], "seq", d)
 
     half = row_count // 2
     send, keep = pl.pallas_call(
-        functools.partial(project_kernel, copies),
+        project_kernel,
         out_shape=(
             jax.ShapeDtypeStruct((half, out_count), jnp.bfloat16),
             jax.ShapeDtypeStruct((half, out_count), jnp.float32),
@@ -375,7 +378,7 @@
     ringed = REACH * row_count * chan_count
     fits = (
         seq_count == 2 * group_count
-        and group_count in (2, 4, 8)
+        and group_count == 4
         and seq_count * long_filter.shape[1] <= REACH * row_count
         and long_filter.shape[1] <= width
         and width == 128

time: 34.1 us -> 32.2 us (0.944)
  starting transfers between devices: 16.8 us -> 15.2 us
    ppermute x12 -> x10, starting transfers between devices: 16.8 us -> 15.2 us  [swapped(): lax.ppermute(array, axis, [(i, i ^ flip) for i in range(lax.axis_size(axi...]
    ppermute x12 -> x10, waiting for transfers between devices: 12 us -> 11.8 us  [swapped(): lax.ppermute(array, axis, [(i, i ^ flip) for i in range(lax.axis_size(axi...]
  transfers between devices with their start and end apart: 12 -> 10, of which waited for: 6 -> 6; matrix products, arithmetic and copies ran while one was open for 0% -> 0% of each run, Pallas kernels for 5% -> 5%
where the time goes in v4:
time: 32.2 us; the launch traced here: 32 us
  starting transfers between devices  15.2 us (47%)
  waiting for transfers between devices  11.8 us (37%)
  Pallas kernels  4.27 us (13%)
  other arithmetic  0.74 us (2%)
    ppermute x10, starting transfers between devices, swapped(): lax.ppermute(array, axis, [(i, i ^ flip) for i in range(lax.axis_size(axi...  15.2 us
    ppermute x10, waiting for transfers between devices, swapped(): lax.ppermute(array, axis, [(i, i ^ flip) for i in range(lax.axis_size(axi...  11.8 us
    pallas_call x1, Pallas kernels, exchange_form(): pl.pallas_call(ready_kernel, out_shape=(jax.ShapeDtypeStruct((row_count,...  1.69 us
    pallas_call x1, Pallas kernels, exchange_form(): pl.pallas_call(gate_kernel, out_shape=[jax.ShapeDtypeStruct((rows_sent, w...  1.33 us
    pallas_call x1, Pallas kernels, exchange_form(): pl.pallas_call(functools.partial(filter_kernel, copies, lags), out_shape=...  0.73 us
    convert_element_type x1, other arithmetic, exchange_form(): return (kept + far.astype(jnp.float32)).astype(jnp.bfloat16)  0.7 us
  transfers between devices with their start and end apart: 10, of which 6 were waited for; matrix products, arithmetic and copies ran while one was open for 0% of the time, Pallas kernels for 5%

profile of v4, /device:TPU:0, one launch (start us, length us, event | category | flops | bytes accessed | tf_op | source)
XLA Modules:
  0.0 32.0 jit_solution(14025312386117091472)
XLA Ops:
  0.0 1.3 %gate.1 = (bf16[144,128]{1,0:T(8,128)(2,1)S(1)}, bf16[144,128]{1,0:T(8,128)(2,1)S(1)}, bf16[144,128]{1,0:T(8,128)(2,1)S(1)}, bf16[144,128]{1,0:T(8,128)(2,1)S(1)}, f32[3,4,3]{2,1,0:T(4,128)S(1)}) custom-call(s32[1]{0:T(128)} %bitcast.place_ref.seq_ref, bf16[3,128,512]{2,1,0:T(8,128)(2,1)} %bitcast.3, bf16[3,4,3]{2,1,0:T(4,128)(2,1)} %short_hbm.1, ...), custom_call_target="tpu_custom_call" | custom-call | flops 786432 | bytes 524288 | tf_op jit(solution)/shard_map/gate/pallas_call | solution.py:288
  1.3 3.0 %collective-permute-start = (bf16[144,128]{1,0:T(8,128)(2,1)S(1)}, bf16[144,128]{1,0:T(8,128)(2,1)S(1)}, u32[]{:S(2)}, u32[]{:S(2)}) collective-permute-start(bf16[144,128]{1,0:T(8,128)(2,1)S(1)} %get-tuple-element.22), channel_id=1, source_target_pairs={{0,4},{4,0},{8,12},{12,8},{16,20},{20,16},{24,28},{28,24},{1,5},{5... | collective-permute-start | bytes 110600 | tf_op jit(solution)/shard_map/ppermute | solution.py:271
  4.4 1.6 %collective-permute-start.1 = (bf16[144,128]{1,0:T(8,128)(2,1)S(1)}, bf16[144,128]{1,0:T(8,128)(2,1)S(1)}, u32[]{:S(2)}, u32[]{:S(2)}) collective-permute-start(bf16[144,128]{1,0:T(8,128)(2,1)S(1)} %get-tuple-element.23), channel_id=1, source_target_pairs={{0,8},{4,12},{8,0},{12,4},{16,24},{20,28},{24,16},{28,20},{1,9},{5... | collective-permute-start | bytes 110600 | tf_op jit(solution)/shard_map/ppermute | solution.py:271
  6.0 0.0 collective-permute-start.2
  6.0 0.4 %collective-permute-done.refs_1_ = bf16[144,128]{1,0:T(8,128)(2,1)S(1)} collective-permute-done((bf16[144,128]{1,0:T(8,128)(2,1)S(1)}, bf16[144,128]{1,0:T(8,128)(2,1)S(1)}, u32[]{:S(2)}, u32[]{:S(2)}) %collective-permute-start) | collective-permute-done | bytes 36896 | tf_op jit(solution)/shard_map/ppermute | solution.py:271
  6.3 3.1 %collective-permute-start.3 = (bf16[288,128]{1,0:T(8,128)(2,1)S(1)}, bf16[288,128]{1,0:T(8,128)(2,1)S(1)}, u32[]{:S(2)}, u32[]{:S(2)}) collective-permute-start(bf16[288,128]{1,0:T(8,128)(2,1)S(1)} %pad_maximum_fusion), channel_id=1, source_target_pairs={{0,16},{4,20},{8,24},{12,28},{16,0},{20,4},{24,8},{28,12},{1,17},{... | collective-permute-start | bytes 221192 | tf_op jit(solution)/shard_map/ppermute | solution.py:271
  9.4 0.0 collective-permute-done.1.refs_2_
  9.4 1.7 %collective-permute-done.2.refs_3_ = bf16[144,128]{1,0:T(8,128)(2,1)S(1)} collective-permute-done((bf16[144,128]{1,0:T(8,128)(2,1)S(1)}, bf16[144,128]{1,0:T(8,128)(2,1)S(1)}, u32[]{:S(2)}, u32[]{:S(2)}) %collective-permute-start.2) | collective-permute-done | bytes 36896 | tf_op jit(solution)/shard_map/ppermute | solution.py:271
  11.1 2.3 %collective-permute-start.4 = (bf16[288,128]{1,0:T(8,128)(2,1)S(1)}, bf16[288,128]{1,0:T(8,128)(2,1)S(1)}, u32[]{:S(2)}, u32[]{:S(2)}) collective-permute-start(bf16[288,128]{1,0:T(8,128)(2,1)S(1)} %pad_maximum_fusion.1), channel_id=1, source_target_pairs={{0,16},{4,20},{8,24},{12,28},{16,0},{20,4},{24,8},{28,12},{1,17},{... | collective-permute-start | bytes 221192 | tf_op jit(solution)/shard_map/ppermute | solution.py:271
  13.4 0.0 collective-permute-done.3
  13.4 3.3 %collective-permute-done.4 = bf16[288,128]{1,0:T(8,128)(2,1)S(1)} collective-permute-done((bf16[288,128]{1,0:T(8,128)(2,1)S(1)}, bf16[288,128]{1,0:T(8,128)(2,1)S(1)}, u32[]{:S(2)}, u32[]{:S(2)}) %collective-permute-start.4) | collective-permute-done | bytes 73760 | tf_op jit(solution)/shard_map/ppermute | solution.py:271
  16.8 0.7 %long_filter.1 = (bf16[136,128]{1,0:T(8,128)(2,1)S(1)}, bf16[136,128]{1,0:T(8,128)(2,1)S(1)}, bf16[136,128]{1,0:T(8,128)(2,1)S(1)}, bf16[136,128]{1,0:T(8,128)(2,1)S(1)}) custom-call(s32[1]{0:T(128)} %bitcast.place_ref.seq_ref, f32[3,4,3]{2,1,0:T(4,128)S(1)} %get-tuple-element.18.table_ref, bf16[144,128]{1,0:T(8,128)(2,1)S(1)} %get-tuple-element.21.refs_0_, ...), custom_call_target="tpu_custom_call" | custom-call | flops 117440512 | bytes 524288 | tf_op jit(solution)/shard_map/long_filter/pallas_call | solution.py:331
  17.5 1.0 %collective-permute-start.5 = (bf16[136,128]{1,0:T(8,128)(2,1)S(1)}, bf16[136,128]{1,0:T(8,128)(2,1)S(1)}, u32[]{:S(2)}, u32[]{:S(2)}) collective-permute-start(bf16[136,128]{1,0:T(8,128)(2,1)S(1)} %get-tuple-element.26), channel_id=1, source_target_pairs={{0,4},{4,0},{8,12},{12,8},{16,20},{20,16},{24,28},{28,24},{1,5},{5... | collective-permute-start | bytes 104456 | tf_op jit(solution)/shard_map/ppermute | solution.py:271
  18.5 0.3 collective-permute-start.6
  18.8 2.3 %collective-permute-start.7 = (bf16[136,128]{1,0:T(8,128)(2,1)S(1)}, bf16[136,128]{1,0:T(8,128)(2,1)S(1)}, u32[]{:S(2)}, u32[]{:S(2)}) collective-permute-start(bf16[136,128]{1,0:T(8,128)(2,1)S(1)} %get-tuple-element.28), channel_id=1, source_target_pairs={{0,12},{4,8},{8,4},{12,0},{16,28},{20,24},{24,20},{28,16},{1,13},{... | collective-permute-start | bytes 104456 | tf_op jit(solution)/shard_map/ppermute | solution.py:271
  21.0 1.7 %ready.1 = (f32[128,512]{1,0:T(8,128)S(1)}, bf16[512,2048]{1,0:T(8,128)(2,1)S(1)}) custom-call(bf16[3,128,512]{2,1,0:T(8,128)(2,1)} %bitcast.4, bf16[512,2048]{1,0:T(8,128)(2,1)} %weight_hbm.1, f32[3,4,3]{2,1,0:T(4,128)S(1)} %get-tuple-element.18.table_ref), custom_call_target="tpu_custom_call" | custom-call | flops 393216 | bytes 2490368 | tf_op jit(solution)/shard_map/ready/pallas_call | solution.py:314
  22.7 0.0 collective-permute-done.5.refs_1_
  22.8 0.8 %collective-permute-done.7.refs_3_ = bf16[136,128]{1,0:T(8,128)(2,1)S(1)} collective-permute-done((bf16[136,128]{1,0:T(8,128)(2,1)S(1)}, bf16[136,128]{1,0:T(8,128)(2,1)S(1)}, u32[]{:S(2)}, u32[]{:S(2)}) %collective-permute-start.7) | collective-permute-done | bytes 34848 | tf_op jit(solution)/shard_map/ppermute | solution.py:271
  23.6 0.5 %project.1 = (bf16[64,2048]{1,0:T(8,128)(2,1)S(1)}, f32[64,2048]{1,0:T(8,128)S(1)}) custom-call(s32[1]{0:T(128)} %bitcast.place_ref.seq_ref, s32[1]{0:T(128)} %bitcast.1.place_ref, f32[128,512]{1,0:T(8,128)S(1)} %get-tuple-element.19.query_ref, f32[3,4,3]{2,1,0:T(4,128)S(1)} %get-tuple-element.18.table_ref, ...), custom_call_target="tpu_custom_call" | custom-call | flops 268435456 | bytes 2097152 | tf_op jit(solution)/shard_map/project/pallas_call | solution.py:351
  24.1 0.1 collective-permute-start.8
  24.2 1.5 %collective-permute-done.8 = bf16[64,2048]{1,0:T(8,128)(2,1)S(1)} collective-permute-done((bf16[64,2048]{1,0:T(8,128)(2,1)S(1)}, bf16[64,2048]{1,0:T(8,128)(2,1)S(1)}, u32[]{:S(2)}, u32[]{:S(2)}) %collective-permute-start.8) | collective-permute-done | bytes 262176 | tf_op jit(solution)/shard_map/ppermute | solution.py:271
  25.7 1.6 %collective-permute-start.9 = (bf16[32,2048]{1,0:T(8,128)(2,1)S(1)}, bf16[32,2048]{1,0:T(8,128)(2,1)S(1)}, u32[]{:S(2)}, u32[]{:S(2)}) collective-permute-start(bf16[32,2048]{1,0:T(8,128)(2,1)S(1)} %add_convert_fusion.1), channel_id=1, source_target_pairs={{0,2},{1,3},{2,0},{3,1},{4,6},{5,7},{6,4},{7,5},{8,10},{9,11},{10,... | collective-permute-start | bytes 393224 | tf_op jit(solution)/shard_map/ppermute | solution.py:271
  27.3 4.0 %collective-permute-done.9 = bf16[32,2048]{1,0:T(8,128)(2,1)S(1)} collective-permute-done((bf16[32,2048]{1,0:T(8,128)(2,1)S(1)}, bf16[32,2048]{1,0:T(8,128)(2,1)S(1)}, u32[]{:S(2)}, u32[]{:S(2)}) %collective-permute-start.9) | collective-permute-done | bytes 131104 | tf_op jit(solution)/shard_map/ppermute | solution.py:271
  31.3 0.7 %add_convert_fusion = bf16[32,2048]{1,0:T(8,128)(2,1)} fusion(bf16[32,2048]{1,0:T(8,128)(2,1)S(1)} %collective-permute-done.9, f32[64,2048]{1,0:T(8,128)S(1)} %get-tuple-element.29, bf16[64,2048]{1,0:T(8,128)(2,1)S(1)} %collective-permute-done.8), kind=kLoop, calls=%fused_computation | loop fusion | flops 327680 | bytes 655360 | tf_op jit(solution)/shard_map/convert_element_type | solution.py:369
  (6 shorter events, 0.1 us)
Async XLA Ops:
  1.3 5.0 %collective-permute-start = (bf16[144,128]{1,0:T(8,128)(2,1)S(1)}, bf16[144,128]{1,0:T(8,128)(2,1)S(1)}, u32[]{:S(2)}, u32[]{:S(2)}) collective-permute-start(bf16[144,128]{1,0:T(8,128)(2,1)S(1)} %get-tuple-element.22), channel_id=1, source_target_pairs={{0,4},{4,0},{8,12},{12,8},{16,20},{20,16},{24,28},{28,24},{1,5},{5... | collective-permute-start | bytes 110600 | tf_op jit(solution)/shard_map/ppermute | solution.py:271
  4.4 5.1 %collective-permute-start.1 = (bf16[144,128]{1,0:T(8,128)(2,1)S(1)}, bf16[144,128]{1,0:T(8,128)(2,1)S(1)}, u32[]{:S(2)}, u32[]{:S(2)}) collective-permute-start(bf16[144,128]{1,0:T(8,128)(2,1)S(1)} %get-tuple-element.23), channel_id=1, source_target_pairs={{0,8},{4,12},{8,0},{12,4},{16,24},{20,28},{24,16},{28,20},{1,9},{5... | collective-permute-start | bytes 110600 | tf_op jit(solution)/shard_map/ppermute | solution.py:271
  6.0 5.2 %collective-permute-start.2 = (bf16[144,128]{1,0:T(8,128)(2,1)S(1)}, bf16[144,128]{1,0:T(8,128)(2,1)S(1)}, u32[]{:S(2)}, u32[]{:S(2)}) collective-permute-start(bf16[144,128]{1,0:T(8,128)(2,1)S(1)} %get-tuple-element.24), channel_id=1, source_target_pairs={{0,12},{4,8},{8,4},{12,0},{16,28},{20,24},{24,20},{28,16},{1,13},{... | collective-permute-start | bytes 110600 | tf_op jit(solution)/shard_map/ppermute | solution.py:271
  6.3 7.1 %collective-permute-start.3 = (bf16[288,128]{1,0:T(8,128)(2,1)S(1)}, bf16[288,128]{1,0:T(8,128)(2,1)S(1)}, u32[]{:S(2)}, u32[]{:S(2)}) collective-permute-start(bf16[288,128]{1,0:T(8,128)(2,1)S(1)} %pad_maximum_fusion), channel_id=1, source_target_pairs={{0,16},{4,20},{8,24},{12,28},{16,0},{20,4},{24,8},{28,12},{1,17},{... | collective-permute-start | bytes 221192 | tf_op jit(solution)/shard_map/ppermute | solution.py:271
  11.1 5.6 %collective-permute-start.4 = (bf16[288,128]{1,0:T(8,128)(2,1)S(1)}, bf16[288,128]{1,0:T(8,128)(2,1)S(1)}, u32[]{:S(2)}, u32[]{:S(2)}) collective-permute-start(bf16[288,128]{1,0:T(8,128)(2,1)S(1)} %pad_maximum_fusion.1), channel_id=1, source_target_pairs={{0,16},{4,20},{8,24},{12,28},{16,0},{20,4},{24,8},{28,12},{1,17},{... | collective-permute-start | bytes 221192 | tf_op jit(solution)/shard_map/ppermute | solution.py:271
  17.5 5.3 %collective-permute-start.5 = (bf16[136,128]{1,0:T(8,128)(2,1)S(1)}, bf16[136,128]{1,0:T(8,128)(2,1)S(1)}, u32[]{:S(2)}, u32[]{:S(2)}) collective-permute-start(bf16[136,128]{1,0:T(8,128)(2,1)S(1)} %get-tuple-element.26), channel_id=1, source_target_pairs={{0,4},{4,0},{8,12},{12,8},{16,20},{20,16},{24,28},{28,24},{1,5},{5... | collective-permute-start | bytes 104456 | tf_op jit(solution)/shard_map/ppermute | solution.py:271
  18.5 4.3 %collective-permute-start.6 = (bf16[136,128]{1,0:T(8,128)(2,1)S(1)}, bf16[136,128]{1,0:T(8,128)(2,1)S(1)}, u32[]{:S(2)}, u32[]{:S(2)}) collective-permute-start(bf16[136,128]{1,0:T(8,128)(2,1)S(1)} %get-tuple-element.27), channel_id=1, source_target_pairs={{0,8},{4,12},{8,0},{12,4},{16,24},{20,28},{24,16},{28,20},{1,9},{5... | collective-permute-start | bytes 104456 | tf_op jit(solution)/shard_map/ppermute | solution.py:271
  18.8 4.8 %collective-permute-start.7 = (bf16[136,128]{1,0:T(8,128)(2,1)S(1)}, bf16[136,128]{1,0:T(8,128)(2,1)S(1)}, u32[]{:S(2)}, u32[]{:S(2)}) collective-permute-start(bf16[136,128]{1,0:T(8,128)(2,1)S(1)} %get-tuple-element.28), channel_id=1, source_target_pairs={{0,12},{4,8},{8,4},{12,0},{16,28},{20,24},{24,20},{28,16},{1,13},{... | collective-permute-start | bytes 104456 | tf_op jit(solution)/shard_map/ppermute | solution.py:271
  24.1 1.6 %collective-permute-start.8 = (bf16[64,2048]{1,0:T(8,128)(2,1)S(1)}, bf16[64,2048]{1,0:T(8,128)(2,1)S(1)}, u32[]{:S(2)}, u32[]{:S(2)}) collective-permute-start(bf16[64,2048]{1,0:T(8,128)(2,1)S(1)} %get-tuple-element.30), channel_id=1, source_target_pairs={{0,1},{1,0},{2,3},{3,2},{4,5},{5,4},{6,7},{7,6},{8,9},{9,8},{10,11... | collective-permute-start | bytes 786440 | tf_op jit(solution)/shard_map/ppermute | solution.py:271
  25.7 5.6 %collective-permute-start.9 = (bf16[32,2048]{1,0:T(8,128)(2,1)S(1)}, bf16[32,2048]{1,0:T(8,128)(2,1)S(1)}, u32[]{:S(2)}, u32[]{:S(2)}) collective-permute-start(bf16[32,2048]{1,0:T(8,128)(2,1)S(1)} %add_convert_fusion.1), channel_id=1, source_target_pairs={{0,2},{1,3},{2,0},{3,1},{4,6},{5,7},{6,4},{7,5},{8,10},{9,11},{10,... | collective-permute-start | bytes 393224 | tf_op jit(solution)/shard_map/ppermute | solution.py:271
